TPU v7x, 128 devices: a whole 4x4x4 slice. The times are simulated.
128 devices in a mesh: tok: 16 (over z, x), exp: 8 (over y, core).
Axes of the slice: x: 4, y: 4, z: 4, core: 2. Of those that a mesh axis runs over, the one named last changes fastest.
Arguments:
- tokens: bfloat16 [3072, 2048], P('tok'), may hold values from -6 to 6
- gain_attn: float32 [2048], replicated, may hold values from 0.5 to 1.5
- router_attn: bfloat16 [2048, 8], replicated, may hold values from -0.125 to 0.125
- kv_weight: bfloat16 [2048, 4096], P(None, 'exp')
- query_weight: bfloat16 [8, 2048, 2048], P('exp', None, 'tok')
- out_weight: bfloat16 [8, 2048, 2048], P('exp', 'tok'), may hold values from -0.125 to 0.125
- gain_mlp: float32 [2048], replicated, may hold values from 0.5 to 1.5
- router_mlp: bfloat16 [2048, 8], replicated, may hold values from -0.125 to 0.125
- gate_weight: bfloat16 [8, 2048, 5632], P('exp', None, 'tok'), may hold values from -0.125 to 0.125
- up_weight: bfloat16 [8, 2048, 5632], P('exp', None, 'tok'), may hold values from -0.125 to 0.125
- down_weight: bfloat16 [8, 5632, 2048], P('exp', 'tok'), may hold values from -0.078125 to 0.078125
- routes_attn: int32 [3072, 2], P('tok'), may hold values from 0 to 7, all different within a row; in each aligned block of 192 rows (0 to 191, 192 to 383, ...) at most 96 rows name the same one
- routes_mlp: int32 [3072, 2], P('tok'), may hold values from 0 to 7, all different within a row; in each aligned block of 192 rows (0 to 191, 192 to 383, ...) at most 96 rows name the same one
- lengths: int32 [3], replicated, may hold values from 256 to 1536, as said below
- page_table: int32 [3, 12, 2], replicated, may hold values from 0 to 15, as said below
Outputs:
- mixed: bfloat16 [3072, 2048], P('tok', 'exp')
- kv_pages: bfloat16 [32, 128, 4096], P('tok', None, 'exp')
Inputs may be any that keep to these rules, and one draw needn't show every extreme that they name: `routes_attn`: in each device's block of 192 tokens no expert is named by more than 96 tokens, a bound that some block reaches of them. `routes_mlp`: in each device's block of 192 tokens no expert is named by more than 96 tokens, a bound that some block reaches of them. The lengths sum to 3072; one prompt has exactly 1536 tokens. `page_table`: entry [s, i] holds (owner along tok, slot) of page i of prompt s, its tokens i * 128 to (i + 1) * 128 - 1; existing pages have distinct (owner, slot) pairs; the pages touched by one device's block of 192 tokens have distinct owners, so one block sends at most one page's tokens to an owner; entries past a prompt's last page are 0.
All inputs are finite; a program needn't handle non-finite values.
Results may differ from a plain program's by a relative error of at most 0.015.
The roundings to bfloat16 on the way count: a program that leaves them out, or rounds other values in their place, can miss the bound.
Values may be sent and summed in bfloat16 or wider, within the bound.
A program may use at most 128 MiB of HBM per device.

v0:
```python
import jax
import jax.numpy as jnp
from jax import lax
from jax.sharding import PartitionSpec as P

HD = 128
PAGE = 128


epsilon = 1e-06


def normalize(values, gain):
    return values * lax.rsqrt(jnp.mean(values * values, axis=-1, keepdims=True) + epsilon) * gain


def rotate(values, position):
    half_width = values.shape[-1] // 2
    exponent = jnp.arange(half_width, dtype=jnp.float32) * (2.0 / values.shape[-1])
    frequency = jnp.power(jnp.float32(10000.0), -exponent)
    angles = position.astype(jnp.float32)[:, None] * frequency[None, :]
    cosine = jnp.cos(angles)[:, None, :]
    sine_part = jnp.sin(angles)[:, None, :]
    leading = values[..., :half_width]
    trailing = values[..., half_width:]
    return jnp.concatenate(
        [leading * cosine - trailing * sine_part, trailing * cosine + leading * sine_part], axis=-1
    )


def locate(lengths, number):
    segment_ends = jnp.cumsum(lengths)
    segment_starts = segment_ends - lengths
    segment = jnp.sum((number[:, None] >= segment_ends[None, :]).astype(jnp.int32), axis=1)
    matched = segment[:, None] == jnp.arange(lengths.shape[0], dtype=jnp.int32)[None, :]
    start_of = jnp.sum(jnp.where(matched, segment_starts[None, :], 0), axis=1)
    return (segment, (number - start_of).astype(jnp.int32), start_of)


def pair_gates(logits, routes):
    leading = jnp.take_along_axis(logits, routes[:, 0:1], axis=1)[:, 0]
    trailing = jnp.take_along_axis(logits, routes[:, 1:2], axis=1)[:, 0]
    return (jax.nn.sigmoid(leading - trailing), jax.nn.sigmoid(trailing - leading))


def compact(routes, leading, trailing, expert, capacity):
    count_rows = routes.shape[0]
    chosen = (routes[:, 0] == expert) | (routes[:, 1] == expert)
    weight = jnp.where(routes[:, 0] == expert, leading, 0.0) + jnp.where(
        routes[:, 1] == expert, trailing, 0.0
    )
    ranking = jnp.cumsum(chosen.astype(jnp.int32)) - 1
    slot_rank = jnp.arange(capacity, dtype=jnp.int32)
    matches = chosen[None, :] & (ranking[None, :] == slot_rank[:, None])
    picked = jnp.sum(
        jnp.where(matches, jnp.arange(count_rows, dtype=jnp.int32)[None, :], 0), axis=1
    )
    filled = slot_rank < jnp.sum(chosen.astype(jnp.int32))
    return (picked, jnp.where(filled, jnp.take(weight, picked), 0.0))


def spread_rows(picked, contribution, count_rows):
    placing = (jnp.arange(count_rows, dtype=jnp.int32)[:, None] == picked[None, :]).astype(
        jnp.float32
    )
    return jnp.dot(placing, contribution, precision=lax.Precision.HIGHEST)


def attend(queries, query_number, query_segment, key_heads, value_heads, key_segment):
    query_total = queries.shape[0]
    key_total = key_heads.shape[0]
    query_groups = max(1, query_total // 512)
    query_rows = query_total // query_groups
    key_groups = max(1, key_total // 512)
    key_rows = key_total // key_groups
    score_scale = queries.shape[-1] ** (-0.5)
    heads_here = queries.shape[1]
    key_number = jnp.arange(key_total, dtype=jnp.int32)
    results = []
    for query_group in range(query_groups):
        row_begin = query_group * query_rows
        query_part = queries[row_begin : row_begin + query_rows]
        number_part = query_number[row_begin : row_begin + query_rows]
        segment_part = query_segment[row_begin : row_begin + query_rows]

        def visit(counter, running):
            highest, denominator, summed = running
            first_key = counter * key_rows
            key_part = lax.dynamic_slice_in_dim(key_heads, first_key, key_rows, 0)
            value_part = lax.dynamic_slice_in_dim(value_heads, first_key, key_rows, 0)
            segment_keys = lax.dynamic_slice_in_dim(key_segment, first_key, key_rows, 0)
            number_keys = lax.dynamic_slice_in_dim(key_number, first_key, key_rows, 0)
            allowed = (segment_keys[None, :] == segment_part[:, None]) & (
                number_keys[None, :] <= number_part[:, None]
            )
            scores = (
                jnp.einsum("qhd,khd->hqk", query_part, key_part, preferred_element_type=jnp.float32)
                * score_scale
            )
            scores = jnp.where(allowed[None], scores, -1e30)
            newest = jnp.maximum(highest, jnp.max(scores, axis=2))
            weights = jnp.where(allowed[None], jnp.exp(scores - newest[:, :, None]), 0.0)
            shrink = jnp.exp(highest - newest)
            denominator = denominator * shrink + jnp.sum(weights, axis=2)
            summed = summed * shrink[:, :, None] + jnp.einsum(
                "hqk,khd->hqd",
                weights.astype(jnp.bfloat16),
                value_part,
                preferred_element_type=jnp.float32,
            )
            return (newest, denominator, summed)

        start_state = (
            jnp.full((heads_here, query_rows), -1e30, jnp.float32),
            jnp.zeros((heads_here, query_rows), jnp.float32),
            jnp.zeros((heads_here, query_rows, queries.shape[-1]), jnp.float32),
        )
        highest, denominator, summed = lax.fori_loop(0, key_groups, visit, start_state)
        results.append(jnp.swapaxes((summed / denominator[:, :, None]).astype(jnp.bfloat16), 0, 1))
    return jnp.concatenate(results, axis=0)


def shards(
    tokens,
    gain_attn,
    router_attn,
    kv_weight,
    query_weight,
    out_weight,
    gain_mlp,
    router_mlp,
    gate_weight,
    up_weight,
    down_weight,
    routes_attn,
    routes_mlp,
    lengths,
    page_table,
):
    tok_count = lax.axis_size("tok")
    exp_count = lax.axis_size("exp")
    tok_rank = lax.axis_index("tok")
    exp_rank = lax.axis_index("exp")
    rows_here, model_width = tokens.shape
    head_size = HD
    heads_kv = kv_weight.shape[1] // (2 * head_size)
    heads_here = query_weight.shape[2] // head_size
    capacity = rows_here // 2
    total_tokens = rows_here * tok_count
    page_rows = PAGE
    pages_each = page_table.shape[1]
    slot_count = (total_tokens // page_rows + lengths.shape[0]) // tok_count + 1
    widened = tokens.astype(jnp.float32)
    normed = normalize(widened, gain_attn).astype(jnp.bfloat16)
    own_number = tok_rank * rows_here + jnp.arange(rows_here, dtype=jnp.int32)
    own_segment, own_offset, own_start = locate(lengths, own_number)
    projected_kv = jnp.dot(normed, kv_weight, preferred_element_type=jnp.float32).reshape(
        rows_here, heads_kv, 2, head_size
    )
    rotated = rotate(projected_kv[:, :, 0], own_offset)
    paired = (
        jnp.stack([rotated, projected_kv[:, :, 1]], axis=2)
        .astype(jnp.bfloat16)
        .reshape(rows_here, heads_kv * 2 * head_size)
    )
    entries = jnp.take(
        page_table.reshape(-1, 2), own_segment * pages_each + own_offset // page_rows, axis=0
    )
    owner_of = entries[:, 0]
    slot_of = entries[:, 1]
    placed = owner_of * page_rows + own_offset % page_rows
    selector = (
        jnp.arange(tok_count * page_rows, dtype=jnp.int32)[:, None] == placed[None, :]
    ).astype(jnp.bfloat16)
    outgoing = (
        jnp.dot(selector, paired, preferred_element_type=jnp.float32)
        .astype(jnp.bfloat16)
        .reshape(tok_count, page_rows, -1)
    )
    owner_hits = owner_of[None, :] == jnp.arange(tok_count, dtype=jnp.int32)[:, None]
    slot_sent = jnp.max(jnp.where(owner_hits, slot_of[None, :], 0), axis=1).reshape(tok_count, 1)
    arrived, arrived_slot = (
        lax.all_to_all(outgoing, "tok", split_axis=0, concat_axis=0, tiled=True),
        lax.all_to_all(slot_sent, "tok", split_axis=0, concat_axis=0, tiled=True),
    )
    filing = (
        jnp.arange(slot_count, dtype=jnp.int32)[:, None] == arrived_slot[:, 0][None, :]
    ).astype(jnp.bfloat16)
    kv_pages = (
        jnp.dot(filing, arrived.reshape(tok_count, -1), preferred_element_type=jnp.float32)
        .astype(jnp.bfloat16)
        .reshape(slot_count, page_rows, -1)
    )
    all_heads = lax.all_gather(paired, "exp", axis=1, tiled=True)
    regrouped = lax.all_to_all(
        all_heads.reshape(rows_here, tok_count, heads_here * 2 * head_size),
        "tok",
        split_axis=1,
        concat_axis=0,
        tiled=True,
    )
    regrouped = regrouped.reshape(total_tokens, heads_here, 2, head_size)
    key_heads = regrouped[:, :, 0]
    value_heads = regrouped[:, :, 1]
    key_segment, key_offset, key_start = locate(lengths, jnp.arange(total_tokens, dtype=jnp.int32))
    attn_logits = jnp.dot(normed, router_attn, preferred_element_type=jnp.float32)
    leading, trailing = pair_gates(attn_logits, routes_attn)
    picked, attn_gate = compact(routes_attn, leading, trailing, exp_rank, capacity)
    chosen_rows = jnp.take(normed, picked, axis=0)
    chosen_number = tok_rank * rows_here + picked
    query_full = jnp.dot(
        chosen_rows,
        lax.all_gather(query_weight[0], "tok", axis=1, tiled=True),
        preferred_element_type=jnp.float32,
    )
    chosen_segment, chosen_offset, chosen_start = locate(lengths, chosen_number)
    query_local = rotate(query_full.reshape(capacity, -1, head_size), chosen_offset).astype(
        jnp.bfloat16
    )
    number_copies = jnp.broadcast_to(chosen_number[:, None], (capacity, tok_count))
    query_heads, query_number = (
        lax.all_to_all(query_local, "tok", split_axis=1, concat_axis=0, tiled=True),
        lax.all_to_all(number_copies, "tok", split_axis=1, concat_axis=0, tiled=True),
    )
    query_number = query_number.reshape(-1)
    query_segment, query_offset, query_start = locate(lengths, query_number)
    attended = attend(query_heads, query_number, query_segment, key_heads, value_heads, key_segment)
    returned = lax.all_to_all(
        attended.reshape(tok_count, capacity, heads_here * head_size),
        "tok",
        split_axis=0,
        concat_axis=2,
        tiled=True,
    )
    returned = returned.reshape(capacity, -1)
    mixed_attn = jnp.dot(
        returned,
        lax.all_gather(out_weight[0], "tok", axis=0, tiled=True),
        preferred_element_type=jnp.float32,
    )
    attn_rows = spread_rows(picked, mixed_attn * attn_gate[:, None], rows_here)
    share_width = model_width // exp_count
    first_column = exp_rank * share_width
    attn_total = lax.psum(attn_rows.astype(jnp.bfloat16), "exp").astype(jnp.float32)
    residual = widened + attn_total
    normed_mlp = normalize(residual, gain_mlp).astype(jnp.bfloat16)
    residual_share = lax.dynamic_slice_in_dim(residual, first_column, share_width, 1)
    mlp_logits = jnp.dot(normed_mlp, router_mlp, preferred_element_type=jnp.float32)
    leading_mlp, trailing_mlp = pair_gates(mlp_logits, routes_mlp)
    picked_mlp, mlp_gate = compact(routes_mlp, leading_mlp, trailing_mlp, exp_rank, capacity)
    expert_input = jnp.take(normed_mlp, picked_mlp, axis=0)
    portion = lax.all_gather(expert_input, "tok", axis=0, tiled=True)
    gate_part = jnp.dot(portion, gate_weight[0], preferred_element_type=jnp.float32)
    upward = jnp.dot(portion, up_weight[0], preferred_element_type=jnp.float32)
    hidden = (jax.nn.silu(gate_part) * upward).astype(jnp.bfloat16)
    expert_out = lax.psum_scatter(
        jnp.dot(hidden, down_weight[0], preferred_element_type=jnp.float32).astype(jnp.bfloat16),
        "tok",
        scatter_dimension=0,
        tiled=True,
    ).astype(jnp.float32)
    expert_local = spread_rows(picked_mlp, expert_out * mlp_gate[:, None], rows_here)
    expert_share = lax.psum_scatter(
        expert_local.astype(jnp.bfloat16), "exp", scatter_dimension=1, tiled=True
    ).astype(jnp.float32)
    mixed = (residual_share + expert_share).astype(jnp.bfloat16)
    return (mixed, kv_pages)


def solution(mesh):
    return jax.shard_map(
        shards,
        mesh=mesh,
        in_specs=(
            P("tok", None),
            P(),
            P(),
            P(None, "exp"),
            P("exp", None, "tok"),
            P("exp", "tok", None),
            P(),
            P(),
            P("exp", None, "tok"),
            P("exp", None, "tok"),
            P("exp", "tok", None),
            P("tok", None),
            P("tok", None),
            P(),
            P(),
        ),
        out_specs=(P("tok", "exp"), P("tok", None, "exp")),
        check_vma=False,
    )
```

profile of v0, /device:TPU:0, one launch (start us, length us, event | category | flops | bytes accessed | tf_op | source)
XLA Modules:
  0.0 524.7 jit_solution(327691876324778887)
XLA Ops:
  7.2 1.5 fusion.77
  8.8 1.4 fusion.79
  18.7 8.0 %all-to-all-start = ((s32[96,16,1]{0,2,1:T(1,128)}), s32[96,16,1]{0,2,1:T(1,128)S(1)}, u32[]{:S(2)}, u32[]{:S(2)}) async-start(s32[96,16,1]{0,2,1:T(1,128)} %broadcast_in_dim.247), calls=%async_computation | async-start | bytes 16384 | tf_op jit(solution)/shard_map/all_to_all | solution.py:223
  28.6 1.5 gather_fusion.2
  30.1 1.5 gather_fusion.3
  32.3 11.2 %all-gather.7.cloned.1.call-done = bf16[192,4096]{1,0:T(8,128)(2,1)} async-done(((bf16[192,512]{1,0:T(8,128)(2,1)}), bf16[192,4096]{1,0:T(8,128)(2,1)}) %all-gather.7.cloned.1.call-update) | async-done | bytes 1572880 | tf_op jit(solution)/shard_map/all_gather | solution.py:194
  43.5 2.7 copy.93
  46.2 6.9 %all-to-all-start.1 = ((bf16[192,16,256]{2,0,1:T(8,128)(2,1)}), bf16[192,16,256]{2,0,1:T(8,128)(2,1)S(1)}, u32[]{:S(2)}, u32[]{:S(2)}) async-start(bf16[192,16,256]{2,0,1:T(8,128)(2,1)} %bitcast.202), calls=%async_computation.1 | async-start | bytes 3145728 | tf_op jit(solution)/shard_map/all_to_all | solution.py:195
  54.7 1.3 gather_fusion.4
  56.1 1.3 compare_select_fusion.16
  59.1 25.7 %all-to-all-done.1 = bf16[192,16,256]{2,0,1:T(8,128)(2,1)S(1)} async-done(((bf16[192,16,256]{2,0,1:T(8,128)(2,1)}), bf16[192,16,256]{2,0,1:T(8,128)(2,1)S(1)}, u32[]{:S(2)}, u32[]{:S(2)}) %all-to-all-start.1) | async-done | bytes 1572896 | tf_op jit(solution)/shard_map/all_to_all | solution.py:195
  84.7 1.2 copy-done.3
  85.9 2.4 reshape.595
  88.3 3.5 fusion.139
  91.7 43.1 %all-gather.11.cloned.1.call-done = bf16[1,2048,2048]{2,1,0:T(8,128)(2,1)} async-done(((bf16[1,2048,128]{2,1,0:T(8,128)(2,1)}), bf16[1,2048,2048]{2,1,0:T(8,128)(2,1)}) %all-gather.11.cloned.1.call-update) | async-done | bytes 8388624 | tf_op jit(solution)/shard_map/all_gather | solution.py:213
  134.9 4.9 fusion.84
  140.7 1.0 pad_maximum_fusion
  141.7 5.0 all-to-all-start.2
  146.7 2.7 copy_bitcast_fusion.1
  149.4 10.8 %all-to-all-done.2 = bf16[96,16,128]{2,0,1:T(8,128)(2,1)S(1)} async-done(((bf16[96,16,128]{2,0,1:T(8,128)(2,1)}), bf16[96,16,128]{2,0,1:T(8,128)(2,1)S(1)}, u32[]{:S(2)}, u32[]{:S(2)}) %all-to-all-start.2) | async-done | bytes 393248 | tf_op jit(solution)/shard_map/all_to_all | solution.py:222
  161.0 19.0 %while.54 = (s32[]{:T(128)}, f32[1,512]{1,0:T(1,128)S(1)}, f32[1,512]{1,0:T(1,128)S(1)}, f32[1,512,128]{2,1,0:T(8,128)}, s32[3072]{0:T(1024)S(1)}, /*index=5*/s3...) while((s32[]{:T(128)}, f32[1,512]{1,0:T(1,128)S(1)}, ...), condition=%wide.region_14.16_spmd.clone, body=%wide.region_11.15_spmd.clone.sunk | while | flops 139135488 | bytes 6226191 | solution.py:118
  161.2 1.4 fusion.181
  164.3 1.4 fusion.181
  167.5 1.4 fusion.181
  170.6 1.4 fusion.181
  173.8 1.4 fusion.181
  177.0 1.4 fusion.181
  180.0 1.1 fusion.98
  181.1 14.5 %while.55 = (s32[]{:T(128)}, f32[1,512]{1,0:T(1,128)S(1)}, f32[1,512]{1,0:T(1,128)S(1)}, f32[1,512,128]{2,1,0:T(8,128)S(1)}, s32[3072]{0:T(1024)S(1)}, /*index=5...) while((s32[]{:T(128)}, f32[1,512]{1,0:T(1,128)S(1)}, ...), condition=%wide.region_18.20_spmd.clone, body=%wide.region_15.19_spmd.clone.sunk | while | flops 139135488 | bytes 4128983 | solution.py:118
  181.3 1.3 fusion.188
  183.7 1.3 fusion.188
  186.1 1.3 fusion.188
  188.5 1.3 fusion.188
  191.0 1.3 fusion.188
  193.4 1.3 fusion.188
  195.8 14.5 %while.56 = (s32[]{:T(128)}, f32[1,512]{1,0:T(1,128)S(1)}, f32[1,512]{1,0:T(1,128)S(1)}, f32[1,512,128]{2,1,0:T(8,128)S(1)}, s32[3072]{0:T(1024)S(1)}, /*index=5...) while((s32[]{:T(128)}, f32[1,512]{1,0:T(1,128)S(1)}, ...), condition=%wide.region_22.24_spmd.clone, body=%wide.region_19.23_spmd.clone.sunk | while | flops 139135488 | bytes 4128983 | solution.py:118
  196.0 1.3 fusion.195
  198.4 1.3 fusion.195
  200.8 1.3 fusion.195
  203.3 1.3 fusion.195
  205.7 1.3 fusion.195
  208.1 1.3 fusion.195
  211.3 3.6 all-to-all-start.3
  215.1 9.2 %all-to-all-done.3 = bf16[16,96,128]{2,1,0:T(8,128)(2,1)S(1)} async-done(((bf16[16,96,128]{2,1,0:T(8,128)(2,1)}), bf16[16,96,128]{2,1,0:T(8,128)(2,1)S(1)}, u32[]{:S(2)}, u32[]{:S(2)}) %all-to-all-start.3) | async-done | bytes 393248 | tf_op jit(solution)/shard_map/all_to_all | solution.py:228
  224.5 4.8 fusion.74
  229.3 1.7 convolution_convert_fusion.4
  231.8 58.7 %all-reduce.4.cloned.1.call-done = bf16[192,2048]{1,0:T(8,128)(2,1)} async-done(((bf16[192,2048]{1,0:T(8,128)(2,1)}), bf16[192,2048]{1,0:T(8,128)(2,1)}) %all-reduce.4.cloned.1.call-update) | async-done | bytes 786448 | tf_op jit(solution)/shard_map/psum | solution.py:244
  290.5 2.6 convert_add_fusion
  294.2 1.5 gather_fusion.6
  295.7 1.5 gather_fusion.7
  298.2 1.3 gather_fusion.8
  300.1 0.9 broadcast_select_fusion.6
  301.3 60.5 %all-gather.9.cloned.1.call-done = bf16[1536,2048]{1,0:T(8,128)(2,1)} async-done(((bf16[96,2048]{1,0:T(8,128)(2,1)}), bf16[1536,2048]{1,0:T(8,128)(2,1)}) %all-gather.9.cloned.1.call-update) | async-done | bytes 6291472 | tf_op jit(solution)/shard_map/all_gather | solution.py:252
  361.8 6.6 %fusion.82 = f32[1536,352]{0,1:T(8,128)} fusion(bf16[1536,2048]{1,0:T(8,128)(2,1)} %all-gather.9.cloned.1.call-done, bf16[1,2048,352]{1,2,0:T(8,128)(2,1)S(1)} %copy-done.33), kind=kOutput, calls=%fused_computation.123 | convolution fusion | flops 2214592512 | bytes 9895936 | tf_op jit(solution)/shard_map/dot_general | solution.py:253
  368.4 11.9 %convolution_convert_fusion.1 = bf16[1536,2048]{1,0:T(8,128)(2,1)} fusion(bf16[1,352,2048]{2,1,0:T(8,128)(2,1)S(1)} %copy-done.34, bf16[1536,2048]{1,0:T(8,128)(2,1)} %all-gather.9.cloned.1.call-done, f32[1536,352]{0,1:T(8,128)} %fusion.82, bf16[1,2048,352]{1,2,0:T(8,128)(2,1)} %param.36), kind=kOutput, calls=%fused_computation.104 | convolution fusion | flops 4435574784 | bytes 17629184 | tf_op jit(solution)/shard_map/dot_general | solution.py:257
  381.7 5.3 %all-to-all-start.4 = ((s32[16,1,1]{2,1,0:T(1,128)}), s32[16,1,1]{2,1,0:T(1,128)S(1)}, u32[]{:S(2)}, u32[]{:S(2)}) async-start(s32[16,1,1]{2,1,0:T(1,128)} %copy.66), calls=%async_computation.6 | async-start | bytes 16384 | tf_op jit(solution)/shard_map/all_to_all | solution.py:184
  387.0 2.1 convolution_convert_fusion.2
  389.1 5.4 %all-to-all-done.4 = s32[16,1,1]{2,1,0:T(1,128)S(1)} async-done(((s32[16,1,1]{2,1,0:T(1,128)}), s32[16,1,1]{2,1,0:T(1,128)S(1)}, u32[]{:S(2)}, u32[]{:S(2)}) %all-to-all-start.4) | async-done | bytes 96 | tf_op jit(solution)/shard_map/all_to_all | solution.py:184
  394.5 3.7 all-to-all-start.5
  398.3 83.9 %reduce-scatter.3.cloned.1.call-done = bf16[96,2048]{1,0:T(8,128)(2,1)} async-done(((bf16[1536,2048]{1,0:T(8,128)(2,1)}), bf16[96,2048]{1,0:T(8,128)(2,1)}) %reduce-scatter.3.cloned.1.call-update) | async-done | bytes 393232 | tf_op jit(solution)/shard_map/reduce_scatter | solution.py:256
  482.2 2.8 convolution_convert_fusion.3
  485.4 1.2 copy.76
  487.7 28.4 %reduce-scatter.5.cloned.1.call-done = bf16[192,256]{1,0:T(8,128)(2,1)} async-done(((bf16[192,2048]{1,0:T(8,128)(2,1)}), bf16[192,256]{1,0:T(8,128)(2,1)}) %reduce-scatter.5.cloned.1.call-update) | async-done | bytes 98320 | tf_op jit(solution)/shard_map/reduce_scatter | solution.py:263
  516.2 1.6 add_convert_fusion.1
  (340 shorter events, 47.4 us)
Async XLA Ops:
  7.2 3.0 copy-start
  7.2 36.3 %all-gather.7.cloned.1.call-start = ((), (), s32[]{:S(2)}) async-start(), calls=%async_computation.8 | async-start | bytes 1769472 | tf_op jit(solution)/shard_map/all_gather | solution.py:194
  10.7 0.7 copy-start.35
  10.8 1.1 copy-start.29
  13.5 0.6 copy-start.19
  14.8 2.5 copy-start.16
  15.3 12.3 %copy-start.17 = (s32[192,2]{0,1:T(2,128)S(1)}, s32[192,2]{0,1:T(2,128)}, u32[]{:S(2)}) copy-start(s32[192,2]{0,1:T(2,128)} %param.39) | copy-start | bytes 4612
  15.4 12.3 %copy-start.14 = (bf16[2048,8]{0,1:T(8,128)(2,1)S(1)}, bf16[2048,8]{0,1:T(8,128)(2,1)}, u32[]{:S(2)}) copy-start(bf16[2048,8]{0,1:T(8,128)(2,1)} %param.29) | copy-start | bytes 98308
  16.5 118.3 %all-gather.11.cloned.1.call-start = ((), (), s32[]{:S(2)}) async-start(), calls=%async_computation.13 | async-start | bytes 8912896 | tf_op jit(solution)/shard_map/all_gather | solution.py:213
  18.1 38.1 %copy-start.22 = (s32[96]{0:T(128)}, s32[96]{0:T(128)S(1)}, u32[]{:S(2)}) copy-start(s32[96]{0:T(128)S(1)} %select_reduce_fusion.1) | copy-start | bytes 1156
  18.7 27.5 %all-to-all-start = ((s32[96,16,1]{0,2,1:T(1,128)}), s32[96,16,1]{0,2,1:T(1,128)S(1)}, u32[]{:S(2)}, u32[]{:S(2)}) async-start(s32[96,16,1]{0,2,1:T(1,128)} %broadcast_in_dim.247), calls=%async_computation | async-start | bytes 16384 | tf_op jit(solution)/shard_map/all_to_all | solution.py:223
  26.7 197.8 %all-gather.13.cloned.1.call-start = ((), (), s32[]{:S(2)}) async-start(), calls=%async_computation.14 | async-start | bytes 8912896 | tf_op jit(solution)/shard_map/all_gather | solution.py:238
  27.7 4.0 copy-start.31
  46.2 38.5 %all-to-all-start.1 = ((bf16[192,16,256]{2,0,1:T(8,128)(2,1)}), bf16[192,16,256]{2,0,1:T(8,128)(2,1)S(1)}, u32[]{:S(2)}, u32[]{:S(2)}) async-start(bf16[192,16,256]{2,0,1:T(8,128)(2,1)} %bitcast.202), calls=%async_computation.1 | async-start | bytes 3145728 | tf_op jit(solution)/shard_map/all_to_all | solution.py:195
  84.7 1.2 copy-start.3
  140.7 6.0 %copy-start.4 = (bf16[3072,1,1,128]{3,2,0,1:T(2,128)(2,1)S(1)}, bf16[3072,1,1,128]{3,2,0,1:T(2,128)(2,1)}, u32[]{:S(2)}) copy-start(bf16[3072,1,1,128]{3,2,0,1:T(2,128)(2,1)} %get-tuple-element.762) | copy-start | bytes 2359300
  141.7 18.5 %all-to-all-start.2 = ((bf16[96,16,128]{2,0,1:T(8,128)(2,1)}), bf16[96,16,128]{2,0,1:T(8,128)(2,1)S(1)}, u32[]{:S(2)}, u32[]{:S(2)}) async-start(bf16[96,16,128]{2,0,1:T(8,128)(2,1)} %pad_maximum_fusion), calls=%async_computation.2 | async-start | bytes 786432 | tf_op jit(solution)/shard_map/all_to_all | solution.py:222
  146.7 14.2 %copy-start.10 = (s32[512]{0:T(512)S(1)}, s32[512]{0:T(512)}, u32[]{:S(2)}) copy-start(s32[512]{0:T(512)} %get-tuple-element.1122) | copy-start | bytes 6148
  146.7 14.2 %copy-start.13 = (f32[1,512]{1,0:T(1,128)S(1)}, f32[1,512]{1,0:T(1,128)}, u32[]{:S(2)}) copy-start(f32[1,512]{1,0:T(1,128)} %custom-call.9) | copy-start | bytes 6148
  160.9 20.1 %copy-start.9 = (bf16[512,1,128]{2,0,1:T(8,128)(2,1)S(1)}, bf16[512,1,128]{2,0,1:T(8,128)(2,1)}, u32[]{:S(2)}) copy-start(bf16[512,1,128]{2,0,1:T(8,128)(2,1)} %get-tuple-element.1081) | copy-start | bytes 393220
  161.0 20.1 %copy-start.12 = (f32[1,512]{1,0:T(1,128)S(1)}, f32[1,512]{1,0:T(1,128)}, u32[]{:S(2)}) copy-start(f32[1,512]{1,0:T(1,128)} %custom-call.12) | copy-start | bytes 6148
  161.0 1.9 copy-start.7
  163.5 0.7 copy-start.8
  164.2 1.9 copy-start.7
  166.6 0.7 copy-start.8
  167.3 1.9 copy-start.7
  169.8 0.7 copy-start.8
  170.5 1.9 copy-start.7
  172.9 0.7 copy-start.8
  173.6 1.9 copy-start.7
  176.1 0.7 copy-start.8
  176.8 1.9 copy-start.7
  179.3 0.7 copy-start.8
  181.1 14.7 %copy-start.11 = (f32[1,512]{1,0:T(1,128)S(1)}, f32[1,512]{1,0:T(1,128)}, u32[]{:S(2)}) copy-start(f32[1,512]{1,0:T(1,128)} %custom-call.15) | copy-start | bytes 6148
  210.3 4.6 copy-start.28
  210.4 4.6 copy-start.32
  210.4 14.1 %copy-start.30 = (f32[96]{0:T(128)S(1)}, f32[96]{0:T(128)}, u32[]{:S(2)}) copy-start(f32[96]{0:T(128)} %get-tuple-element.750) | copy-start | bytes 1156
  211.3 12.9 %all-to-all-start.3 = ((bf16[16,96,128]{2,1,0:T(8,128)(2,1)}), bf16[16,96,128]{2,1,0:T(8,128)(2,1)S(1)}, u32[]{:S(2)}, u32[]{:S(2)}) async-start(bf16[16,96,128]{2,1,0:T(8,128)(2,1)} %bitcast.21), calls=%async_computation.3 | async-start | bytes 786432 | tf_op jit(solution)/shard_map/all_to_all | solution.py:228
  214.9 75.6 %all-reduce.4.cloned.1.call-start = ((), (), s32[]{:S(2)}) async-start(), calls=%async_computation.9 | async-start | bytes 1572864 | tf_op jit(solution)/shard_map/psum | solution.py:244
  224.5 4.9 copy-start.23
  229.3 2.5 copy-start.24
  229.3 2.4 copy-start.25
  229.3 61.2 %copy-start.2 = (bf16[192,2048]{1,0:T(8,128)(2,1)S(1)}, bf16[192,2048]{1,0:T(8,128)(2,1)}, u32[]{:S(2)}) copy-start(bf16[192,2048]{1,0:T(8,128)(2,1)} %param.27) | copy-start | bytes 2359300
  231.1 130.7 %all-gather.9.cloned.1.call-start = ((), (), s32[]{:S(2)}) async-start(), calls=%async_computation.10 | async-start | bytes 6684672 | tf_op jit(solution)/shard_map/all_gather | solution.py:252
  231.8 61.4 %copy-start.21 = (f32[2048]{0:T(1024)S(1)}, f32[2048]{0:T(1024)}, u32[]{:S(2)}) copy-start(f32[2048]{0:T(1024)} %param.33) | copy-start | bytes 24580
  290.5 2.6 copy-start.5
  293.1 0.8 copy-start.15
  297.3 0.9 copy-start.18
  298.1 63.7 %copy-start.33 = (bf16[1,2048,352]{1,2,0:T(8,128)(2,1)S(1)}, bf16[1,2048,352]{1,2,0:T(8,128)(2,1)}, u32[]{:S(2)}) copy-start(bf16[1,2048,352]{1,2,0:T(8,128)(2,1)} %param.35) | copy-start | bytes 4325380
  301.0 67.4 %copy-start.34 = (bf16[1,352,2048]{2,1,0:T(8,128)(2,1)S(1)}, bf16[1,352,2048]{2,1,0:T(8,128)(2,1)}, u32[]{:S(2)}) copy-start(bf16[1,352,2048]{2,1,0:T(8,128)(2,1)} %param.37) | copy-start | bytes 4325380
  301.0 181.2 %reduce-scatter.3.cloned.1.call-start = ((), (), s32[]{:S(2)}) async-start(), calls=%async_computation.11 | async-start | bytes 6684672 | tf_op jit(solution)/shard_map/reduce_scatter | solution.py:256
  380.2 0.7 copy-start.20
  380.2 0.7 copy-start.26
  380.2 6.8 %copy-start.6 = (bf16[192,512]{1,0:T(8,128)(2,1)S(1)}, bf16[192,512]{1,0:T(8,128)(2,1)}, u32[]{:S(2)}) copy-start(bf16[192,512]{1,0:T(8,128)(2,1)} %convert_element_type.123) | copy-start | bytes 589828
  380.3 6.8 %copy-start.27 = (s32[192]{0:T(256)S(1)}, s32[192]{0:T(256)}, u32[]{:S(2)}) copy-start(s32[192]{0:T(256)} %get-tuple-element.783) | copy-start | bytes 2308
  381.7 12.8 %all-to-all-start.4 = ((s32[16,1,1]{2,1,0:T(1,128)}), s32[16,1,1]{2,1,0:T(1,128)S(1)}, u32[]{:S(2)}, u32[]{:S(2)}) async-start(s32[16,1,1]{2,1,0:T(1,128)} %copy.66), calls=%async_computation.6 | async-start | bytes 16384 | tf_op jit(solution)/shard_map/all_to_all | solution.py:184
  394.5 90.9 %all-to-all-start.5 = ((bf16[16,128,512]{2,1,0:T(8,128)(2,1)}), bf16[16,128,512]{2,1,0:T(8,128)(2,1)S(1)}, u32[]{:S(2)}, u32[]{:S(2)}) async-start(bf16[16,128,512]{2,1,0:T(8,128)(2,1)} %bitcast.52), calls=%async_computation.7 | async-start | bytes 4194304 | tf_op jit(solution)/shard_map/all_to_all | solution.py:183
  398.2 117.9 %reduce-scatter.5.cloned.1.call-start = ((), (), s32[]{:S(2)}) async-start(), calls=%async_computation.12 | async-start | bytes 884736 | tf_op jit(solution)/shard_map/reduce_scatter | solution.py:263
  486.5 31.3 %copy-start.1 = (bf16[2048,512]{1,0:T(8,128)(2,1)S(1)}, bf16[2048,512]{1,0:T(8,128)(2,1)}, u32[]{:S(2)}) copy-start(bf16[2048,512]{1,0:T(8,128)(2,1)} %param.30) | copy-start | bytes 6291460
Sparse Core Ops, SparseCore 0:
  16.6 26.8 all-gather.6
  45.6 89.1 all-gather.10
  137.0 72.2 all-gather.12
  231.2 59.2 all-reduce.3
  301.1 60.6 all-gather.8
  380.4 101.7 reduce-scatter.2
  485.1 31.0 reduce-scatter.4
where the time goes:
time: 526 us; the launch traced here: 525 us
  waiting for transfers between devices  338 us (64%)
  matrix products  70.3 us (13%)
  local copies, waits for them, and re-layouts  40.2 us (8%)
  starting transfers between devices  32.9 us (6%)
  other arithmetic  26.9 us (5%)
  between operations  15 us (3%)
    reduce_scatter x1, waiting for transfers between devices, shards(): lax.psum_scatter(jnp.dot(hidden, down_weight[0], preferred_element_type=j...  83.9 us
    all_gather x1, waiting for transfers between devices, shards(): portion = lax.all_gather(expert_input, 'tok', axis=0, tiled=True)  60.5 us
    psum x1, waiting for transfers between devices, shards(): lax.psum(attn_rows.astype(jnp.bfloat16), 'exp').astype(jnp.float32)  58.7 us
    all_gather x1, waiting for transfers between devices, shards(): lax.all_gather(query_weight[0], 'tok', axis=1, tiled=True)  43.1 us
    reduce_scatter x1, waiting for transfers between devices, shards(): lax.psum_scatter(expert_local.astype(jnp.bfloat16), 'exp', scatter_dimens...  28.4 us
    all_to_all x1, waiting for transfers between devices, shards(): lax.all_to_all(all_heads.reshape(rows_here, tok_count, heads_here * 2 * h...  25.7 us
    dot_general x18, matrix products, visit(): jnp.einsum('qhd,khd->hqk', query_part, key_part, preferred_element_type=j...  23.6 us
    dot_general x1, matrix products, shards(): jnp.dot(hidden, down_weight[0], preferred_element_type=jnp.float32)  11.9 us
  transfers between devices with their start and end apart: 13, of which 10 were waited for; matrix products, arithmetic and copies ran while one was open for 16% of the time, Pallas kernels for 0%

commit v1 on v0

v1 whole, which is shorter than its diff:
```python
import jax
import jax.numpy as jnp
from jax import lax
from jax.experimental import pallas as pl
from jax.experimental.pallas import tpu as pltpu
from jax.sharding import PartitionSpec as P

HD = 128
PAGE = 128
TOK_DEV = 192
TOKENS = 3072
D = 2048
FF_DEV = 352
HALF = 1024
QUARTER = 512
BLK = 384
SLOTS_BLK = 192
epsilon = 1e-06
MESH = pl.DeviceIdType.MESH
ANY = pl.BlockSpec(memory_space=pl.ANY)
VMEM = pl.BlockSpec(memory_space=pltpu.VMEM)
DIMS = ("z", "x", "y")
GATHER_ORDERS = (("z", "y", "x"), ("x", "z", "y"), ("y", "x", "z"))
SUM_ORDERS = (("x", "y", "z"), ("y", "z", "x"), ("z", "x", "y"))


class Place:
    def __init__(self):
        self.t = lax.axis_index("tok")
        self.e = lax.axis_index("exp")
        self.at = {"z": self.t // 4, "x": self.t % 4, "y": self.e // 2}
        self.c = self.e % 2

    def device(self, **moved):
        at = {**self.at, "c": self.c, **moved}
        return {"tok": at["z"] * 4 + at["x"], "exp": at["y"] * 2 + at["c"]}

    def step(self, dim, delta):
        return (self.at[dim] + delta) % 4

    def sibling(self):
        return self.device(c=1 - self.c)

    def neighbours(self):
        found = [self.sibling()]
        for dim in DIMS:
            found.append(self.device(**{dim: self.step(dim, 1)}))
            found.append(self.device(**{dim: self.step(dim, 3)}))
        return found


class Copies:
    def __init__(self, send, recv):
        self.send, self.recv, self.count, self.started = send, recv, 0, []

    def start(self, src, dst, device):
        number = self.count
        self.count += 1
        copy = pltpu.make_async_remote_copy(
            src_ref=src,
            dst_ref=dst,
            send_sem=self.send.at[number],
            recv_sem=self.recv.at[number],
            device_id=device,
            device_id_type=MESH,
        )
        copy.start()
        self.started.append(copy)
        return copy

    def drain(self):
        for copy in self.started:
            copy.wait_send()


def greet(partners):
    barrier = pltpu.get_barrier_semaphore()
    for partner in partners:
        pl.semaphore_signal(barrier, inc=1, device_id=partner, device_id_type=MESH)
    pl.semaphore_wait(barrier, len(partners))


def torus_gather(place, copies, out):
    c = place.c
    full = pl.ds(pl.multiple_of(c * HALF, HALF), HALF)
    first = pl.ds(pl.multiple_of(c * HALF, QUARTER), QUARTER)
    second = pl.ds(pl.multiple_of(c * HALF + QUARTER, QUARTER), QUARTER)
    sibling = place.sibling()
    handed = []

    def part(colour, stage, at, features):
        order = GATHER_ORDERS[colour]
        where = []
        for dim in DIMS:
            if dim in order[:stage]:
                where.append(slice(None))
            elif dim == order[stage]:
                where.append(at)
            else:
                where.append(place.at[dim])
        return out.at[(*where, colour, slice(None), features)]

    def send(colour, stage, at, features, device):
        region = part(colour, stage, at, features)
        return copies.start(region, region, device)

    def open_stage(colour, stage):
        dim = GATHER_ORDERS[colour][stage]
        right = place.device(**{dim: place.step(dim, 1)})
        left = place.device(**{dim: place.step(dim, 3)})
        own = place.at[dim]
        pair = (send(colour, stage, own, full, right), send(colour, stage, own, full, left))
        if stage == 2:
            handed.append(send(colour, stage, own, full, sibling))
        return (right, left, *pair)

    opened = [open_stage(colour, 0) for colour in range(3)]
    for stage in range(3):
        forwards = []
        for colour in range(3):
            dim = GATHER_ORDERS[colour][stage]
            right, left, to_right, to_left = opened[colour]
            to_right.wait_recv()
            on_right = send(colour, stage, place.step(dim, 3), first, right)
            if stage == 2:
                handed.append(send(colour, stage, place.step(dim, 3), full, sibling))
            to_left.wait_recv()
            on_left = send(colour, stage, place.step(dim, 1), second, left)
            if stage == 2:
                handed.append(send(colour, stage, place.step(dim, 1), full, sibling))
            forwards.append((on_right, on_left))
        for colour in range(3):
            dim = GATHER_ORDERS[colour][stage]
            on_right, on_left = forwards[colour]
            on_right.wait_recv()
            on_left.wait_recv()
            if stage < 2:
                opened[colour] = open_stage(colour, stage + 1)
            else:
                handed.append(send(colour, stage, place.step(dim, 2), full, sibling))
    for copy in handed:
        copy.wait_recv()


GATHER_COPIES = 3 * (3 * 4 + 4)


def sum_buffers(rows, width):
    shapes = []
    for lead in ((4, 4), (4,), ()):
        for size in (width // 2, width // 2, width, width):
            shapes.append(pltpu.VMEM((3, *lead, rows, size), jnp.bfloat16))
    return shapes


SUM_COPIES = 3 * 3 * 6


def torus_sum(place, copies, held, buffers):
    width = held.shape[-1]
    first, second, full = pl.ds(0, width // 2), pl.ds(width // 2, width // 2), slice(None)
    finals = []

    def part(colour, stage, at, features, inner=None):
        order = SUM_ORDERS[colour]
        where, inner = [], list(inner) if inner is not None else None
        for dim in DIMS:
            if dim in order[:stage]:
                where.append(place.at[dim])
            elif dim == order[stage]:
                where.append(at)
            else:
                where.append(slice(None) if inner is None else inner.pop(0))
        return held.at[(*where, colour, slice(None), features)]

    def each(stage, body):
        if stage == 0:

            def wide(number, carry):
                body((number // 4, number % 4))
                return carry

            lax.fori_loop(0, 16, wide, 0)
        elif stage == 1:
            for number in range(4):
                body((number,))
        else:
            body(())

    def add(colour, stage, at, features, arrived):
        def one(inner):
            target = part(colour, stage, at, features, inner)
            total = target[...].astype(jnp.float32)
            for ref in arrived:
                total = total + ref.at[(colour, *inner)][...].astype(jnp.float32)
            target[...] = total.astype(jnp.bfloat16)

        each(stage, one)

    def open_stage(colour, stage):
        dim = SUM_ORDERS[colour][stage]
        from_left, from_right, last_left, last_right = buffers[4 * stage : 4 * stage + 4]
        right = place.device(**{dim: place.step(dim, 1)})
        left = place.device(**{dim: place.step(dim, 3)})
        far, after, before = place.step(dim, 2), place.step(dim, 1), place.step(dim, 3)

        def lot(ref, features):
            return ref.at[colour] if features is None else ref.at[(colour, Ellipsis, features)]

        far_right = copies.start(part(colour, stage, far, first), lot(from_left, None), right)
        far_left = copies.start(part(colour, stage, far, second), lot(from_right, None), left)
        raw_right = copies.start(part(colour, stage, after, second), lot(last_left, second), right)
        raw_left = copies.start(part(colour, stage, before, first), lot(last_right, first), left)
        return (right, left, far_right, far_left, raw_right, raw_left)

    opened = [open_stage(colour, 0) for colour in range(3)]
    for stage in range(3):
        from_left, from_right, last_left, last_right = buffers[4 * stage : 4 * stage + 4]
        closing = []
        for colour in range(3):
            dim = SUM_ORDERS[colour][stage]
            right, left, far_right, far_left, raw_right, raw_left = opened[colour]
            after, before = place.step(dim, 1), place.step(dim, 3)
            far_right.wait_recv()
            add(colour, stage, after, first, (from_left,))
            sum_right = copies.start(
                part(colour, stage, after, first), last_left.at[(colour, Ellipsis, first)], right
            )
            far_left.wait_recv()
            add(colour, stage, before, second, (from_right,))
            sum_left = copies.start(
                part(colour, stage, before, second), last_right.at[(colour, Ellipsis, second)], left
            )
            closing.append((sum_right, sum_left))
        for colour in range(3):
            dim = SUM_ORDERS[colour][stage]
            raw_right, raw_left = opened[colour][4:]
            for copy in (raw_right, raw_left, *closing[colour]):
                copy.wait_recv()
            if stage < 2:
                add(colour, stage, place.at[dim], full, (last_left, last_right))
                opened[colour] = open_stage(colour, stage + 1)
            else:
                own = part(colour, stage, place.at[dim], full)[...].astype(jnp.float32)
                finals.append(
                    own
                    + last_left.at[colour][...].astype(jnp.float32)
                    + last_right.at[colour][...].astype(jnp.float32)
                )
    return finals


def spread_kernel(
    tokens_ref, gain_ref, kv_ref, routes_ref, wo_ref, wd_ref,
    out, wkv_out, routes_out, wo_out, wd_out,
    rows, send, recv, local,
):
    place = Place()
    copies = Copies(send, recv)
    t, e, c, y = place.t, place.e, place.c, place.at["y"]
    others = [{"tok": (t + delta) % 16, "exp": e} for delta in range(1, 16)]
    across = [{"tok": t, "exp": (e + delta) % 8} for delta in range(1, 8)]
    values = tokens_ref[y].astype(jnp.float32)
    scale = lax.rsqrt(jnp.mean(values * values, axis=-1, keepdims=True) + epsilon)
    rows[...] = (values * scale * gain_ref[...]).astype(jnp.bfloat16)
    half = pl.ds(pl.multiple_of(c * HALF, HALF), HALF)
    own = pltpu.make_async_copy(
        rows.at[:, :, half],
        out.at[place.at["z"], place.at["x"], y, :, :, half],
        local.at[0],
    )
    own.start()
    own_routes = pltpu.make_async_copy(routes_ref, routes_out.at[t], local.at[1])
    own_routes.start()
    greet(others + across)
    own.wait()
    side = Copies(send.at[pl.ds(GATHER_COPIES, 40)], recv.at[pl.ds(GATHER_COPIES, 40)])
    sibling = place.sibling()
    source = t // 2
    columns = pl.ds(pl.multiple_of((t % 2) * 256, 256), 256)
    mine = pl.ds(pl.multiple_of(c * HALF, HALF), HALF)
    theirs = pl.ds(pl.multiple_of((1 - c) * HALF, HALF), HALF)
    fan_send = [send.at[GATHER_COPIES + 40 + number] for number in range(7)]
    fan_recv = recv.at[GATHER_COPIES + 40]

    def fan(number, lines, device):
        return pltpu.make_async_remote_copy(
            src_ref=kv_ref.at[lines, columns],
            dst_ref=wkv_out.at[lines, :],
            send_sem=fan_send[number],
            recv_sem=fan_recv,
            device_id=device,
            device_id_type=MESH,
        )

    def fans():
        made = [fan(0, theirs, sibling)]
        for delta in range(1, 4):
            for core in range(2):
                made.append(
                    fan(
                        len(made),
                        pl.ds(core * HALF, HALF),
                        place.device(y=(y + delta) % 4, c=core),
                    )
                )
        return made

    @pl.when(e == source)
    def _():
        for copy in fans():
            copy.start()
        keep = pltpu.make_async_copy(kv_ref.at[mine, columns], wkv_out.at[mine, :], local.at[2])
        keep.start()
        keep.wait()

    routed = [
        side.start(routes_ref, routes_out.at[t], device) for device in others
    ]
    given_wo = side.start(wo_ref.at[:, theirs], wo_out, sibling)
    given_wd = []
    for number in range(4):
        lanes = pl.ds(pl.multiple_of(number * 512 + (1 - c) * 256, 256), 256)
        given_wd.append(side.start(wd_ref.at[:, lanes], wd_out.at[:, pl.ds(number * 256, 256)], sibling))
    torus_gather(place, copies, out)

    @pl.when(e != source)
    def _():
        fan(0, mine, sibling).wait_recv()

    shared = side.start(wkv_out.at[mine, :], wkv_out.at[mine, :], sibling)

    shared.wait_recv()
    own_routes.wait()
    for copy in routed + [given_wo] + given_wd:
        copy.wait_recv()

    @pl.when(e == source)
    def _():
        for copy in fans():
            copy.wait_send()

    copies.drain()
    side.drain()


def attend_kernel(
    scalars, x_ref, wqr_ref, wkv_ref, cos_ref, sin_ref, aux_ref, out_ref, keys, values
):
    block = pl.program_id(0)
    expert = scalars[8]
    rows = x_ref[...]
    query_part = jnp.dot(rows, wqr_ref[...], preferred_element_type=jnp.float32)
    kv_part = jnp.dot(rows, wkv_ref[...], preferred_element_type=jnp.float32)
    cosine, sine = cos_ref[...], sin_ref[...]

    def rotate(v):
        return (v * cosine + pltpu.roll(v, 64, 1) * sine).astype(jnp.bfloat16)

    here = pl.ds(pl.multiple_of(block * BLK, BLK), BLK)
    keys[here, :] = rotate(kv_part[:, :HD])
    values[here, :] = kv_part[:, HD:].astype(jnp.bfloat16)
    queries = rotate(query_part[:, :HD])
    logits = query_part[:, HD:]
    first, second, start = aux_ref[:, 0:1], aux_ref[:, 1:2], aux_ref[:, 4:5]
    chosen = (first == expert) | (second == expert)
    other = first + second - expert
    lane = lax.broadcasted_iota(jnp.int32, (BLK, HD), 1)
    own_logit = jnp.sum(jnp.where(lane == expert, logits, 0.0), axis=1, keepdims=True)
    other_logit = jnp.sum(jnp.where(lane == other, logits, 0.0), axis=1, keepdims=True)
    gate = jnp.where(chosen, 1.0 / (1.0 + jnp.exp(other_logit - own_logit)), 0.0)
    row_number = lax.broadcasted_iota(jnp.int32, (BLK, BLK), 0)
    column_number = lax.broadcasted_iota(jnp.int32, (BLK, BLK), 1)
    below = jnp.where(row_number >= column_number, 1.0, 0.0).astype(jnp.bfloat16)
    flags = jnp.broadcast_to(jnp.where(chosen, 1.0, 0.0), (BLK, HD)).astype(jnp.bfloat16)
    rank = jnp.dot(below, flags, preferred_element_type=jnp.float32)[:, 0:1] - 1.0
    slot = lax.broadcasted_iota(jnp.int32, (BLK, SLOTS_BLK), 1).astype(jnp.float32)
    placing = jnp.where(chosen & (rank == slot), 1.0, 0.0).astype(jnp.bfloat16)
    inside = lax.broadcasted_iota(jnp.int32, (BLK, HD), 0)
    digits = jnp.where(
        lane == 0,
        inside // 16,
        jnp.where(lane == 1, inside % 16, jnp.where(lane == 2, start // 64, jnp.where(lane == 3, start % 64, 0))),
    ).astype(jnp.float32).astype(jnp.bfloat16)
    across = (((0,), (0,)), ((), ()))
    picked = lax.dot_general(placing, queries, across, preferred_element_type=jnp.float32).astype(jnp.bfloat16)
    told = lax.dot_general(placing, digits, across, preferred_element_type=jnp.float32)
    highest_key = told[:, 0:1] * 16.0 + told[:, 1:2] + (block * BLK).astype(jnp.float32)
    lowest_key = told[:, 2:3] * 64.0 + told[:, 3:4]
    key_lane = lax.broadcasted_iota(jnp.int32, (SLOTS_BLK, BLK), 1)

    def visit(tile, carry):
        highest, denominator, summed = carry
        there = pl.ds(pl.multiple_of(tile * BLK, BLK), BLK)
        scores = lax.dot_general(
            picked, keys[there, :], (((1,), (1,)), ((), ())), preferred_element_type=jnp.float32
        ) * (HD**-0.5)
        number = (key_lane + tile * BLK).astype(jnp.float32)
        scores = jnp.where((number >= lowest_key) & (number <= highest_key), scores, -1e30)
        newest = jnp.maximum(highest, jnp.max(scores, axis=1, keepdims=True))
        weights = jnp.exp(scores - newest)
        shrink = jnp.exp(highest - newest)
        denominator = denominator * shrink + jnp.sum(weights, axis=1, keepdims=True)
        summed = summed * shrink + jnp.dot(
            weights.astype(jnp.bfloat16), values[there, :], preferred_element_type=jnp.float32
        )
        return newest, denominator, summed

    _, denominator, summed = lax.fori_loop(
        scalars[block],
        block + 1,
        visit,
        (
            jnp.full((SLOTS_BLK, 1), -1e30, jnp.float32),
            jnp.zeros((SLOTS_BLK, 1), jnp.float32),
            jnp.zeros((SLOTS_BLK, HD), jnp.float32),
        ),
    )
    attended = (summed / denominator).astype(jnp.bfloat16)
    dense = jnp.dot(placing, attended, preferred_element_type=jnp.float32)
    out_ref[...] = (dense * gate).astype(jnp.bfloat16)


def middle_kernel(
    heads_ref, wo_ref, wo_pair_ref, tokens_ref, gain_ref,
    out, residual_out,
    paired, weights, held, shared, squares, rows, residual, send, recv, local, *buffers,
):
    place = Place()
    t, e, c, y = place.t, place.e, place.c, place.at["y"]
    across = [{"tok": t, "exp": (e + delta) % 8} for delta in range(1, 8)]
    around = [device for number, device in enumerate(place.neighbours()) if number in (1, 2, 3, 4)]
    greet(around + across)
    copies = Copies(send, recv)
    sibling = place.sibling()
    half = pl.ds(pl.multiple_of(c * HALF, HALF), HALF)
    given = copies.start(heads_ref, paired, sibling)
    weights[0:HD, :] = wo_ref[:, half]
    weights[HD : 2 * HD, :] = wo_pair_ref[...]
    given.wait_recv()

    def project(number, carry):
        lines = pl.ds(pl.multiple_of(number * TOK_DEV, TOK_DEV), TOK_DEV)
        both = jnp.concatenate([heads_ref[lines, :], paired[lines, :]], axis=1)
        part = jnp.dot(both, weights[...], preferred_element_type=jnp.float32)
        held[number // 4, number % 4] = part.astype(jnp.bfloat16).reshape(4, 3, 16, HALF)
        return carry

    lax.fori_loop(0, 16, project, 0)
    sums = torus_sum(place, copies, held, buffers)
    square = []
    for colour in range(3):
        value = tokens_ref[y, colour, :, half].astype(jnp.float32) + sums[colour]
        residual[colour] = value
        square.append(jnp.sum(value * value, axis=-1, keepdims=True))
        shared[colour] = jnp.broadcast_to(square[colour], (16, HD))
    swapped = copies.start(shared, squares, sibling)
    for colour in range(3):
        for number in range(4):
            rows_here = pl.ds(colour * 16, 16)
            residual_out_part = residual[colour, :, number * 256 : (number + 1) * 256]
            buffers[-1][number, rows_here, :] = residual_out_part
    pieces = buffers[-1]
    base = send.shape[0] - 4

    def piece(number, sender):
        return pltpu.make_async_remote_copy(
            src_ref=pieces.at[number],
            dst_ref=residual_out.at[sender],
            send_sem=send.at[base + number],
            recv_sem=recv.at[base + sender],
            device_id={"tok": t, "exp": 4 * c + number},
            device_id_type=MESH,
        )

    for number in range(4):

        @pl.when(4 * c + number == e)
        def _():
            keep = pltpu.make_async_copy(pieces.at[number], residual_out.at[y], local.at[1])
            keep.start()
            keep.wait()

        @pl.when(4 * c + number != e)
        def _():
            piece(number, y).start()

    swapped.wait_recv()
    for colour in range(3):
        total = square[colour] + squares[colour][:, 0:1]
        scale = lax.rsqrt(total * (1.0 / D) + epsilon)
        rows[colour] = (residual[colour] * scale * gain_ref[:, half]).astype(jnp.bfloat16)
    own = pltpu.make_async_copy(
        rows, out.at[place.at["z"], place.at["x"], y, :, :, half], local.at[0]
    )
    own.start()
    own.wait()
    torus_gather(place, copies, out)
    for sender in range(4):
        itself = (y == sender) & (c == e // 4)

        @pl.when(jnp.logical_not(itself))
        def _():
            piece(0, sender).wait_recv()

    for number in range(4):

        @pl.when(4 * c + number != e)
        def _():
            piece(number, y).wait_send()

    copies.drain()


def hidden_kernel(scalars, x_ref, wg_ref, wu_ref, router_ref, aux_ref, out_ref):
    expert = scalars[8]
    rows = x_ref[...]
    logits = jnp.dot(rows, router_ref[...], preferred_element_type=jnp.float32)
    first, second = aux_ref[:, 2:3], aux_ref[:, 3:4]
    chosen = (first == expert) | (second == expert)
    other = first + second - expert
    lane = lax.broadcasted_iota(jnp.int32, (BLK, HD), 1)
    own_logit = jnp.sum(jnp.where(lane == expert, logits, 0.0), axis=1, keepdims=True)
    other_logit = jnp.sum(jnp.where(lane == other, logits, 0.0), axis=1, keepdims=True)
    gate = jnp.where(chosen, 1.0 / (1.0 + jnp.exp(other_logit - own_logit)), 0.0)
    opened = jnp.dot(rows, wg_ref[...], preferred_element_type=jnp.float32)
    upward = jnp.dot(rows, wu_ref[...], preferred_element_type=jnp.float32)
    hidden = opened / (1.0 + jnp.exp(-opened)) * upward
    out_ref[...] = (hidden * gate).astype(jnp.bfloat16)


def last_kernel(
    hidden_ref, wd_ref, wd_pair_ref, residual_ref,
    out_ref,
    paired, held, send, recv, *buffers,
):
    place = Place()
    c = place.c
    greet(place.neighbours())
    copies = Copies(send, recv)
    given = copies.start(hidden_ref, paired, place.sibling())
    given.wait_recv()

    def project(number, carry):
        lines = pl.ds(pl.multiple_of(number * TOK_DEV, TOK_DEV), TOK_DEV)
        own, pair = hidden_ref[lines, :], paired[lines, :]
        for at in range(4):
            lanes = pl.ds(pl.multiple_of(at * 512 + c * 256, 256), 256)
            part = jnp.dot(own, wd_ref[:, lanes], preferred_element_type=jnp.float32)
            part += jnp.dot(
                pair, wd_pair_ref[:, at * 256 : (at + 1) * 256], preferred_element_type=jnp.float32
            )
            held[number // 4, number % 4, at] = part.astype(jnp.bfloat16).reshape(3, 64, 256)
        return carry

    lax.fori_loop(0, 16, project, 0)
    sums = torus_sum(place, copies, held, buffers)
    for colour in range(3):
        lines = slice(colour * 64, (colour + 1) * 64)
        out_ref[lines, :] = (residual_ref[lines, :] + sums[colour]).astype(jnp.bfloat16)
    copies.drain()


def shards(
    tokens,
    gain_attn,
    router_attn,
    kv_weight,
    query_weight,
    out_weight,
    gain_mlp,
    router_mlp,
    gate_weight,
    up_weight,
    down_weight,
    routes_attn,
    routes_mlp,
    lengths,
    page_table,
):
    t = lax.axis_index("tok")
    e = lax.axis_index("exp")
    bf16 = jnp.bfloat16
    struct = jax.ShapeDtypeStruct
    tokens_parts = tokens.reshape(4, 3, 16, D)
    own_routes = jnp.concatenate([routes_attn, routes_mlp], axis=1).T
    own_routes = jnp.pad(own_routes, ((0, 4), (0, 64)))
    spread_count = GATHER_COPIES + 40 + 8
    gathered, wkv, routes, wo_pair, wd_pair = pl.pallas_call(
        spread_kernel,
        out_shape=(
            struct((4, 4, 4, 3, 16, D), bf16),
            struct((D, 256), bf16),
            struct((16, 8, 256), jnp.int32),
            struct((HD, HALF), bf16),
            struct((FF_DEV, HALF), bf16),
        ),
        in_specs=[VMEM, VMEM, ANY, ANY, ANY, ANY],
        out_specs=(ANY,) * 5,
        scratch_shapes=[
            pltpu.VMEM((3, 16, D), bf16),
            pltpu.SemaphoreType.DMA((spread_count,)),
            pltpu.SemaphoreType.DMA((spread_count,)),
            pltpu.SemaphoreType.DMA((3,)),
        ],
        compiler_params=pltpu.CompilerParams(collective_id=0, has_side_effects=True),
        name="spread",
    )(tokens_parts, gain_attn.reshape(1, 1, D), kv_weight, own_routes, out_weight[0], down_weight[0])
    h1 = gathered.reshape(TOKENS, D)

    ends = jnp.cumsum(lengths)
    starts = ends - lengths
    number = jnp.arange(TOKENS, dtype=jnp.int32)
    start_of = jnp.zeros((TOKENS,), jnp.int32)
    for prompt in range(1, lengths.shape[0]):
        start_of = jnp.where(number >= starts[prompt], starts[prompt], start_of)
    exponent = jnp.arange(64, dtype=jnp.float32) * (2.0 / HD)
    frequency = jnp.power(jnp.float32(10000.0), -exponent)
    angles = (number - start_of).astype(jnp.float32)[:, None] * frequency[None, :]
    cosine, sine = jnp.cos(angles), jnp.sin(angles)
    cos_table = jnp.concatenate([cosine, cosine], axis=1)
    sin_table = jnp.concatenate([-sine, sine], axis=1)
    aux = jnp.concatenate(
        [
            jnp.swapaxes(routes[:, :4, :TOK_DEV], 1, 2).reshape(TOKENS, 4),
            start_of[:, None],
            jnp.zeros((TOKENS, 3), jnp.int32),
        ],
        axis=1,
    )
    scalars = jnp.concatenate([start_of[::BLK] // BLK, e.reshape(1), jnp.zeros((7,), jnp.int32)]).astype(jnp.int32)
    wqr = jnp.concatenate([query_weight[0], jnp.pad(router_attn, ((0, 0), (0, HD - 8)))], axis=1)
    steps = TOKENS // BLK

    def whole(shape):
        return pl.BlockSpec(shape, lambda i, s: (0,) * len(shape))

    def lines(width):
        return pl.BlockSpec((BLK, width), lambda i, s: (i, 0))

    heads = pl.pallas_call(
        attend_kernel,
        out_shape=struct((TOKENS, HD), bf16),
        grid_spec=pltpu.PrefetchScalarGridSpec(
            num_scalar_prefetch=1,
            grid=(steps,),
            in_specs=[lines(D), whole((D, 256)), whole((D, 256)), lines(HD), lines(HD), lines(8)],
            out_specs=lines(HD),
            scratch_shapes=[pltpu.VMEM((TOKENS, HD), bf16), pltpu.VMEM((TOKENS, HD), bf16)],
        ),
        name="attend",
    )(scalars, h1, wqr, wkv, cos_table, sin_table, aux)

    pages = jnp.arange(page_table.shape[1], dtype=jnp.int32)
    exists = (pages[None, :] * PAGE < lengths[:, None]) & (page_table[:, :, 0] == t)
    page_rows, page_offsets, page_valid = [], [], []
    within = jnp.arange(PAGE, dtype=jnp.int32)
    for slot in range(2):
        here = (exists & (page_table[:, :, 1] == slot)).astype(jnp.int32)
        first_offset = jnp.sum(here * pages[None, :] * PAGE)
        length = jnp.sum(here * lengths[:, None])
        begin = jnp.sum(here * starts[:, None])
        offset = first_offset + within
        page_offsets.append(offset)
        page_valid.append(offset < length)
        page_rows.append(jnp.clip(begin + offset, 0, TOKENS - 1))
    page_offset = jnp.concatenate(page_offsets)
    page_kv = jnp.dot(
        jnp.take(h1, jnp.concatenate(page_rows), axis=0, mode="clip"),
        kv_weight,
        preferred_element_type=jnp.float32,
    ).reshape(2 * PAGE, 2, 2, HD)
    page_angles = page_offset.astype(jnp.float32)[:, None] * frequency[None, :]
    page_cos, page_sin = jnp.cos(page_angles)[:, None, :], jnp.sin(page_angles)[:, None, :]
    low, high = page_kv[:, :, 0, :64], page_kv[:, :, 0, 64:]
    page_keys = jnp.concatenate([low * page_cos - high * page_sin, high * page_cos + low * page_sin], axis=-1)
    page_kv = jnp.stack([page_keys, page_kv[:, :, 1]], axis=2).reshape(2 * PAGE, 512)
    kv_pages = jnp.where(jnp.concatenate(page_valid)[:, None], page_kv, 0.0).astype(bf16).reshape(2, PAGE, 512)

    middle_count = 2 + SUM_COPIES + GATHER_COPIES + 4
    gathered, residual = pl.pallas_call(
        middle_kernel,
        out_shape=(struct((4, 4, 4, 3, 16, D), bf16), struct((4, 48, 256), jnp.float32)),
        in_specs=[VMEM] * 5,
        out_specs=(ANY, ANY),
        scratch_shapes=[
            pltpu.VMEM((TOKENS, HD), bf16),
            pltpu.VMEM((2 * HD, HALF), bf16),
            pltpu.VMEM((4, 4, 4, 3, 16, HALF), bf16),
            pltpu.VMEM((3, 16, HD), jnp.float32),
            pltpu.VMEM((3, 16, HD), jnp.float32),
            pltpu.VMEM((3, 16, HALF), bf16),
            pltpu.VMEM((3, 16, HALF), jnp.float32),
            pltpu.SemaphoreType.DMA((middle_count,)),
            pltpu.SemaphoreType.DMA((middle_count,)),
            pltpu.SemaphoreType.DMA((2,)),
            *sum_buffers(16, HALF),
            pltpu.VMEM((4, 48, 256), jnp.float32),
        ],
        compiler_params=pltpu.CompilerParams(collective_id=1, has_side_effects=True),
        name="middle",
    )(heads, out_weight[0], wo_pair, tokens_parts, gain_mlp.reshape(1, D))
    h2 = gathered.reshape(TOKENS, D)

    hidden = pl.pallas_call(
        hidden_kernel,
        out_shape=struct((TOKENS, FF_DEV), bf16),
        grid_spec=pltpu.PrefetchScalarGridSpec(
            num_scalar_prefetch=1,
            grid=(steps,),
            in_specs=[lines(D), whole((D, FF_DEV)), whole((D, FF_DEV)), whole((D, HD)), lines(8)],
            out_specs=lines(FF_DEV),
        ),
        name="hidden",
    )(scalars, h2, gate_weight[0], up_weight[0], jnp.pad(router_mlp, ((0, 0), (0, HD - 8))), aux)

    last_count = 1 + SUM_COPIES
    mixed = pl.pallas_call(
        last_kernel,
        out_shape=struct((TOK_DEV, 256), bf16),
        in_specs=[VMEM] * 4,
        out_specs=VMEM,
        scratch_shapes=[
            pltpu.VMEM((TOKENS, FF_DEV), bf16),
            pltpu.VMEM((4, 4, 4, 3, 64, 256), bf16),
            pltpu.SemaphoreType.DMA((last_count,)),
            pltpu.SemaphoreType.DMA((last_count,)),
            *sum_buffers(64, 256),
        ],
        compiler_params=pltpu.CompilerParams(collective_id=2, has_side_effects=True),
        name="last",
    )(hidden, down_weight[0], wd_pair, residual.reshape(TOK_DEV, 256))
    return (mixed, kv_pages)


def solution(mesh):
    return jax.shard_map(
        shards,
        mesh=mesh,
        in_specs=(
            P("tok", None),
            P(),
            P(),
            P(None, "exp"),
            P("exp", None, "tok"),
            P("exp", "tok", None),
            P(),
            P(),
            P("exp", None, "tok"),
            P("exp", None, "tok"),
            P("exp", "tok", None),
            P("tok", None),
            P("tok", None),
            P(),
            P(),
        ),
        out_specs=(P("tok", "exp"), P("tok", None, "exp")),
        check_vma=False,
    )
```

time: 526 us -> 324 us (0.62)
  waiting for transfers between devices: 338 us -> 0 us
  Pallas kernels: 0 us -> 273 us
  matrix products: 70.3 us -> 1.53 us
  starting transfers between devices: 32.9 us -> 0 us
  local copies, waits for them, and re-layouts: 40.2 us -> 20.5 us
  between operations: 15 us -> 0.91 us
    pallas_call x0 -> x5, Pallas kernels: none -> 273 us  [the longest x1 87.3 us: shards(): pl.pallas_call(middle_kernel, out_shape=(struct((4, 4, 4, 3, 16, D), bf16...]
    all_gather x4 -> x0, waiting for transfers between devices: 115 us -> none  [the longest x1 60.5 us: shards(): portion = lax.all_gather(expert_input, 'tok', axis=0, tiled=True)]
    reduce_scatter x2 -> x0, waiting for transfers between devices: 112 us -> none  [the longest x1 83.9 us: shards(): lax.psum_scatter(jnp.dot(hidden, down_weight[0], preferred_element_type=j...]
    dot_general x47 -> x1, matrix products: 70.3 us -> 1.53 us  [shards(): jnp.dot(jnp.take(h1, jnp.concatenate(page_rows), axis=0, mode='clip'), kv...]
    psum x1 -> x0, waiting for transfers between devices: 58.7 us -> none  [shards(): lax.psum(attn_rows.astype(jnp.bfloat16), 'exp').astype(jnp.float32)]
    all_to_all x6 -> x0, waiting for transfers between devices: 51 us -> none  [the longest x1 25.7 us: shards(): lax.all_to_all(all_heads.reshape(rows_here, tok_count, heads_here * 2 * h...]
    all_to_all x6 -> x0, starting transfers between devices: 32.4 us -> none  [the longest x1 7.99 us: shards(): lax.all_to_all(number_copies, 'tok', split_axis=1, concat_axis=0, tiled=T...]
    reduce_sum x29 -> x1, other arithmetic: 9.31 us -> 1.51 us  [shards(): length = jnp.sum(here * lengths[:, None])]
  transfers between devices with their start and end apart: 13 -> 0, of which waited for: 10 -> 0; matrix products, arithmetic and copies ran while one was open for 16% -> 0% of each run, Pallas kernels for 0% -> 0%
where the time goes in v1:
time: 324 us; the launch traced here: 323 us
  Pallas kernels  273 us (84%)
  other arithmetic  27.6 us (9%)
  local copies, waits for them, and re-layouts  20.5 us (6%)
    pallas_call x1, Pallas kernels, shards(): pl.pallas_call(middle_kernel, out_shape=(struct((4, 4, 4, 3, 16, D), bf16...  87.3 us
    pallas_call x1, Pallas kernels, shards(): pl.pallas_call(spread_kernel, out_shape=(struct((4, 4, 4, 3, 16, D), bf16...  73.5 us
    pallas_call x1, Pallas kernels, shards(): pl.pallas_call(last_kernel, out_shape=struct((TOK_DEV, 256), bf16), in_sp...  55.3 us
    pallas_call x1, Pallas kernels, shards(): pl.pallas_call(attend_kernel, out_shape=struct((TOKENS, HD), bf16), grid_...  34.5 us
    pallas_call x1, Pallas kernels, shards(): pl.pallas_call(hidden_kernel, out_shape=struct((TOKENS, FF_DEV), bf16), g...  22.2 us
    gather x1, local copies, waits for them, and re-layouts, shards(): jnp.take(h1, jnp.concatenate(page_rows), axis=0, mode='clip')  8.7 us

profile of v1, /device:TPU:0, one launch (start us, length us, event | category | flops | bytes accessed | tf_op | source)
XLA Modules:
  0.0 323.4 jit_solution(10860160932539490387)
XLA Ops:
  0.6 0.8 slice_compare_fusion.2
  1.4 0.7 bitcast_and_fusion
  2.2 0.8 reduce-window.9
  3.0 0.7 bitcast_subtract_fusion
  3.6 1.5 select_reduce_fusion.3
  5.1 2.5 add_clamp_fusion
  7.6 0.7 add_bitcast_fusion
  8.3 0.6 pad.11.routes_ref
  8.9 73.5 %spread.1 = (bf16[4,4,4,3,16,2048]{5,4,3,2,1,0:T(8,128)(2,1)}, bf16[2048,256]{1,0:T(8,128)(2,1)}, s32[16,8,256]{2,1,0:T(8,128)}, bf16[128,1024]{1,0:T(8,128)(2,1)}, bf16[352,1024]{1,0:T(8,128)(2,1)}) custom-call(bf16[4,3,16,2048]{3,2,1,0:T(8,128)(2,1)} %bitcast.48, f32[1,1,2048]{2,1,0:T(1,128)} %bitcast.57, bf16[2048,512]{1,0:T(8,128)(2,1)} %kv_ref.1, ...), custom_call_target="tpu_custom_call" | custom-call | tf_op jit(solution)/shard_map/spread/pallas_call | solution.py:589
  82.5 0.0 copy-start
  82.5 8.7 %gather_fusion = bf16[256,2048]{1,0:T(8,128)(2,1)S(1)} fusion(bf16[3072,2048]{1,0:T(8,128)(2,1)} %bitcast.41, s32[1024]{0:T(1024)S(1)} %pad_clamp_fusion), kind=kCustom, calls=%fused_computation | custom fusion | bytes 2098176 | tf_op jit(solution)/shard_map/jit(_take)/gather | solution.py:669
  91.2 0.0 copy-done
  91.2 1.5 fusion.5
  92.7 1.4 reshape.181
  94.1 0.7 fusion.3
  94.8 1.2 iota_add_fusion
  96.1 0.5 multiply_cosine_fusion.1
  96.6 0.3 multiply_subtract_fusion
  96.9 0.3 pad_maximum_fusion.3
  97.2 0.3 slice.43
  97.5 0.5 pad_maximum_fusion.2
  98.1 0.1 reshape.182
  98.2 2.5 broadcast_compare_fusion
  100.7 0.8 select_convert_fusion
  101.5 0.6 fusion.4
  102.1 1.3 subtract_convert_fusion
  103.4 6.0 %fusion.2 = (f32[3072,64]{1,0:T(8,128)S(1)}, f32[3072,64]{1,0:T(8,128)S(1)}, f32[3072,64]{1,0:T(8,128)S(1)}) fusion(f32[64]{0:T(128)S(1)} %negate_power_fusion, f32[3072]{0:T(1024)S(1)} %get-tuple-element.38), kind=kLoop, calls=%fused_computation.10 | loop fusion | flops 393216 | bytes 2371840 | tf_op jit(solution)/shard_map/neg | solution.py:622
  109.4 0.0 copy-start.6
  109.4 1.7 pad_maximum_fusion.1.sin_ref
  111.1 0.0 copy-done.6
  111.2 0.1 reshape.177
  111.3 1.3 compare_select_fusion.1
  112.6 0.1 pad.26.clone
  112.6 0.1 add_add_fusion
  112.7 1.6 copy.41.aux_ref
  114.4 0.0 copy-start.4
  114.4 0.0 copy-start.3
  114.4 1.6 pad_maximum_fusion.cos_ref
  116.0 0.1 slice.32
  116.1 0.6 pad_add_fusion.1.scalars
  116.7 0.0 copy-done.4
  116.7 0.3 copy.39
  116.9 0.0 copy-done.3
  116.9 1.2 fusion.1.wqr_ref
  118.1 34.5 %attend.1.heads_ref = bf16[3072,128]{1,0:T(8,128)(2,1)} custom-call(s32[16]{0:T(128)} %pad_add_fusion.1.scalars, bf16[3072,2048]{1,0:T(8,128)(2,1)} %bitcast.42, bf16[2048,256]{1,0:T(8,128)(2,1)} %fusion.1.wqr_ref, bf16[2048,256]{1,0:T(8,128)(2,1)} %get-tuple-element.10.wkv_ref, f32[3072,128]{1,0:T(8,128)} %pad_maximum_fusion.cos_ref, ...), custom_call_target="tpu_custom_call" | custom-call | tf_op jit(solution)/shard_map/attend/pallas_call | solution.py:641
  152.6 0.0 copy-start.1
  152.6 87.3 %middle.1 = (bf16[4,4,4,3,16,2048]{5,4,3,2,1,0:T(8,128)(2,1)}, f32[4,48,256]{2,1,0:T(8,128)}) custom-call(bf16[3072,128]{1,0:T(8,128)(2,1)} %attend.1.heads_ref, bf16[128,2048]{1,0:T(8,128)(2,1)} %bitcast.51, bf16[128,1024]{1,0:T(8,128)(2,1)} %get-tuple-element.12.wo_pair_ref, bf16[4,3,16,2048]{3,2,1,0:T(8,128)(2,1)} %bitcast.49, f32[1,2048]{1,0:T(1,128)} %bitcast.58), custom_call_target="tpu_custom_call" | custom-call | tf_op jit(solution)/shard_map/middle/pallas_call | solution.py:681
  239.9 0.0 copy-start.2
  239.9 0.0 copy-done.1
  240.0 1.6 copy.42
  241.5 0.0 copy-start.5
  241.5 0.0 copy-done.2
  241.5 1.6 copy.43
  243.1 0.0 copy-done.5
  243.1 0.3 copy.44
  243.4 0.9 pad.13.router_ref
  244.3 22.2 %hidden.1.hidden_ref = bf16[3072,352]{1,0:T(8,128)(2,1)} custom-call(s32[16]{0:T(128)} %pad_add_fusion.1.scalars, bf16[3072,2048]{1,0:T(8,128)(2,1)} %bitcast.43, bf16[2048,352]{1,0:T(8,128)(2,1)} %bitcast.44, bf16[2048,352]{1,0:T(8,128)(2,1)} %bitcast.45, bf16[2048,128]{1,0:T(8,128)(2,1)} %pad.13.router_ref, s32[3072,8]{1,0:T(8,128)} %copy.41.aux_ref), custom_call_target="tpu_custom_call" | custom-call | tf_op jit(solution)/shard_map/hidden/pallas_call | solution.py:705
  266.6 55.3 %last.1 = bf16[192,256]{1,0:T(8,128)(2,1)} custom-call(bf16[3072,352]{1,0:T(8,128)(2,1)} %hidden.1.hidden_ref, bf16[352,2048]{1,0:T(8,128)(2,1)} %bitcast.47, bf16[352,1024]{1,0:T(8,128)(2,1)} %get-tuple-element.14.wd_pair_ref, f32[192,256]{1,0:T(8,128)} %bitcast.56), custom_call_target="tpu_custom_call" | custom-call | tf_op jit(solution)/shard_map/last/pallas_call | solution.py:718
  321.8 1.5 copy.58
  (11 shorter events, 0.1 us)
Async XLA Ops:
  82.5 8.7 %copy-start = (bf16[2048,512]{1,0:T(8,128)(2,1)S(1)}, bf16[2048,512]{1,0:T(8,128)(2,1)}, u32[]{:S(2)}) copy-start(bf16[2048,512]{1,0:T(8,128)(2,1)} %kv_ref.1) | copy-start | bytes 6291460
  109.4 1.7 copy-start.6
  114.4 2.3 copy-start.4
  114.4 2.6 copy-start.3
  152.6 87.4 %copy-start.1 = (bf16[1,2048,352]{1,2,0:T(8,128)(2,1)S(1)}, bf16[1,2048,352]{1,2,0:T(8,128)(2,1)}, u32[]{:S(2)}) copy-start(bf16[1,2048,352]{1,2,0:T(8,128)(2,1)} %param.23) | copy-start | bytes 4325380
  239.9 1.6 copy-start.2
  241.5 1.6 copy-start.5

commit v2 on v1

v2 whole, which is shorter than its diff:
```python
import jax
import jax.numpy as jnp
import numpy as np
from jax import lax
from jax.experimental import pallas as pl
from jax.experimental.pallas import tpu as pltpu
from jax.sharding import PartitionSpec as P

HD = 128
PAGE = 128
TOK_DEV = 192
TOKENS = 3072
D = 2048
FF_DEV = 352
HALF = 1024
QUARTER = 512
BLK = 384
SLOTS_BLK = 192
epsilon = 1e-06
MESH = pl.DeviceIdType.MESH
ANY = pl.BlockSpec(memory_space=pl.ANY)
VMEM = pl.BlockSpec(memory_space=pltpu.VMEM)
DIMS = ("z", "x", "y")
GATHER_ORDERS = (("z", "y", "x"), ("x", "z", "y"), ("y", "x", "z"))
SUM_ORDERS = (("x", "y", "z"), ("y", "z", "x"), ("z", "x", "y"))


class Place:
    def __init__(self):
        self.t = lax.axis_index("tok")
        self.e = lax.axis_index("exp")
        self.at = {"z": self.t // 4, "x": self.t % 4, "y": self.e // 2}
        self.c = self.e % 2

    def device(self, **moved):
        at = {**self.at, "c": self.c, **moved}
        return {"tok": at["z"] * 4 + at["x"], "exp": at["y"] * 2 + at["c"]}

    def step(self, dim, delta):
        return (self.at[dim] + delta) % 4

    def sibling(self):
        return self.device(c=1 - self.c)

    def neighbours(self):
        found = [self.sibling()]
        for dim in DIMS:
            found.append(self.device(**{dim: self.step(dim, 1)}))
            found.append(self.device(**{dim: self.step(dim, 3)}))
        return found


class Copies:
    def __init__(self, send, recv):
        self.send, self.recv, self.count, self.started = send, recv, 0, []

    def start(self, src, dst, device):
        number = self.count
        self.count += 1
        copy = pltpu.make_async_remote_copy(
            src_ref=src,
            dst_ref=dst,
            send_sem=self.send.at[number],
            recv_sem=self.recv.at[number],
            device_id=device,
            device_id_type=MESH,
        )
        copy.start()
        self.started.append(copy)
        return copy

    def drain(self):
        for copy in self.started:
            copy.wait_send()


def greet(partners):
    barrier = pltpu.get_barrier_semaphore()
    for partner in partners:
        pl.semaphore_signal(barrier, inc=1, device_id=partner, device_id_type=MESH)
    pl.semaphore_wait(barrier, len(partners))


def torus_gather(place, copies, out, hooks=()):
    c = place.c
    full = pl.ds(pl.multiple_of(c * HALF, HALF), HALF)
    first = pl.ds(pl.multiple_of(c * HALF, QUARTER), QUARTER)
    second = pl.ds(pl.multiple_of(c * HALF + QUARTER, QUARTER), QUARTER)
    sibling = place.sibling()
    handed = []
    colours = range(3)

    def hook(number):
        if number < len(hooks):
            hooks[number]()

    def send(colour, at, features, device):
        where = [at.get(dim, place.at[dim]) for dim in DIMS]
        region = out.at[(*where, colour, slice(None), features)]
        return copies.start(region, region, device)

    def pair(dim):
        return place.device(**{dim: place.step(dim, 1)}), place.device(**{dim: place.step(dim, 3)})

    def give(colour, at):
        handed.append(send(colour, at, full, sibling))

    everything = slice(None)
    begun = []
    for colour in colours:
        right, left = pair(GATHER_ORDERS[colour][0])
        begun.append((send(colour, {}, full, right), send(colour, {}, full, left)))
    hook(0)
    passed = []
    for colour in colours:
        dim = GATHER_ORDERS[colour][0]
        right, left = pair(dim)
        begun[colour][0].wait_recv()
        on_right = send(colour, {dim: place.step(dim, 3)}, first, right)
        begun[colour][1].wait_recv()
        on_left = send(colour, {dim: place.step(dim, 1)}, second, left)
        passed.append((on_right, on_left))

    groups = [{} for _ in colours]
    ahead = [{} for _ in colours]

    def place_of(colour, group, line):
        low, middle, high = GATHER_ORDERS[colour]
        return {low: everything, middle: place.step(middle, group), high: place.step(high, line)}

    def open_group(colour, group):
        right, left = pair(GATHER_ORDERS[colour][2])
        at = place_of(colour, group, 0)
        groups[colour][group] = (send(colour, at, full, right), send(colour, at, full, left))
        give(colour, at)

    def turn_group(colour, group):
        right, left = pair(GATHER_ORDERS[colour][2])
        to_right, to_left = groups[colour][group]
        to_right.wait_recv()
        on_right = send(colour, place_of(colour, group, 3), first, right)
        give(colour, place_of(colour, group, 3))
        to_left.wait_recv()
        on_left = send(colour, place_of(colour, group, 1), second, left)
        give(colour, place_of(colour, group, 1))
        ahead[colour][group] = (on_right, on_left)

    def close_group(colour, group):
        for copy in ahead[colour][group]:
            copy.wait_recv()
        give(colour, place_of(colour, group, 2))

    second_begun = []
    for colour in colours:
        for copy in passed[colour]:
            copy.wait_recv()
        low, middle, _ = GATHER_ORDERS[colour]
        right, left = pair(middle)
        at = {low: everything}
        second_begun.append(
            (
                send(colour, at, first, right),
                send(colour, at, second, left),
                send(colour, at, second, right),
                send(colour, at, first, left),
            )
        )
        open_group(colour, 0)
    hook(1)
    second_passed = []
    for colour in colours:
        low, middle, _ = GATHER_ORDERS[colour]
        right, left = pair(middle)
        near_right, near_left, rest_right, rest_left = second_begun[colour]
        near_right.wait_recv()
        on_right = send(colour, {low: everything, middle: place.step(middle, 3)}, first, right)
        near_left.wait_recv()
        on_left = send(colour, {low: everything, middle: place.step(middle, 1)}, second, left)
        second_passed.append((on_right, on_left))
    for colour in colours:
        second_begun[colour][2].wait_recv()
        open_group(colour, 3)
        second_begun[colour][3].wait_recv()
        open_group(colour, 1)
    for colour in colours:
        turn_group(colour, 0)
    hook(2)
    for colour in colours:
        for copy in second_passed[colour]:
            copy.wait_recv()
        open_group(colour, 2)
    for colour in colours:
        turn_group(colour, 3)
    for colour in colours:
        turn_group(colour, 1)
        close_group(colour, 0)
    hook(3)
    for colour in colours:
        turn_group(colour, 2)
        close_group(colour, 3)
        close_group(colour, 1)
    for colour in colours:
        close_group(colour, 2)
    for copy in handed:
        copy.wait_recv()


GATHER_COPIES = 3 * (4 + 6 + 16 + 16)


def sum_buffers(rows, width):
    shapes = []
    for lead in ((4, 4), (4,), ()):
        for size in (width // 2, width // 2, width, width):
            shapes.append(pltpu.VMEM((3, *lead, rows, size), jnp.bfloat16))
    return shapes


SUM_COPIES = 3 * 36


def torus_sum(place, copies, held, buffers):
    width = held.shape[-1]
    first, second, full = pl.ds(0, width // 2), pl.ds(width // 2, width // 2), slice(None)
    colours = range(3)
    order_of_groups = (2, 1, 3, 0)

    def part(colour, at, features):
        where = [at[dim] if dim in at else place.at[dim] for dim in DIMS]
        return held.at[(*where, colour, slice(None), features)]

    def add(colour, at, spread_over, features, arrived):
        def one(at, pieces):
            target = part(colour, at, features)
            total = target[...].astype(jnp.float32)
            for piece in pieces:
                total = total + piece[...].astype(jnp.float32)
            target[...] = total.astype(jnp.bfloat16)

        if spread_over is None:
            one(at, arrived)
        else:

            def step(number, carry):
                one({**at, spread_over: number}, [piece.at[number] for piece in arrived])
                return carry

            lax.fori_loop(0, 4, step, 0)

    def lanes(ref, features):
        return ref if features is None else ref.at[(Ellipsis, features)]

    class Ring:
        def __init__(self, colour, dim, fixed, spread_over, refs):
            self.colour, self.dim, self.fixed, self.spread_over, self.refs = colour, dim, fixed, spread_over, refs
            self.right = place.device(**{dim: place.step(dim, 1)})
            self.left = place.device(**{dim: place.step(dim, 3)})

        def at(self, delta):
            return {**self.fixed, self.dim: place.step(self.dim, delta)}

        def send(self, delta, features, target, device):
            return copies.start(part(self.colour, self.at(delta), features), target, device)

        def far(self):
            self.far_right = self.send(2, first, self.refs[0], self.right)
            self.far_left = self.send(2, second, self.refs[1], self.left)

        def raw_right_part(self):
            self.raw_right = self.send(1, second, lanes(self.refs[2], second), self.right)

        def raw_left_part(self):
            self.raw_left = self.send(3, first, lanes(self.refs[3], first), self.left)

        def pass_right(self):
            self.far_right.wait_recv()
            add(self.colour, self.at(1), self.spread_over, first, [self.refs[0]])
            self.sum_right = self.send(1, first, lanes(self.refs[2], first), self.right)

        def pass_left(self):
            self.far_left.wait_recv()
            add(self.colour, self.at(3), self.spread_over, second, [self.refs[1]])
            self.sum_left = self.send(3, second, lanes(self.refs[3], second), self.left)

        def arrive(self):
            for copy in (self.raw_right, self.raw_left, self.sum_right, self.sum_left):
                copy.wait_recv()

        def close(self):
            self.arrive()
            add(self.colour, self.at(0), self.spread_over, full, [self.refs[2], self.refs[3]])

    rings, seconds, thirds = [], [], []
    for colour in colours:
        wide, middle, narrow = SUM_ORDERS[colour]
        by_group = []
        for number, group in enumerate(order_of_groups):
            refs = [ref.at[colour, number] for ref in buffers[0:4]]
            fixed = {middle: place.step(middle, group), narrow: slice(None)}
            by_group.append(Ring(colour, wide, fixed, narrow, refs))
        rings.append(by_group)
        refs = [ref.at[colour] for ref in buffers[4:8]]
        seconds.append(Ring(colour, middle, {narrow: slice(None)}, narrow, refs))
        thirds.append(Ring(colour, narrow, {}, None, [ref.at[colour] for ref in buffers[8:12]]))

    def open_ring(ring):
        ring.far()
        ring.raw_right_part()
        ring.raw_left_part()

    for number in range(2):
        for colour in colours:
            open_ring(rings[colour][number])
    for number in range(4):
        for colour in colours:
            rings[colour][number].pass_right()
            rings[colour][number].pass_left()
        if number + 2 < 4:
            for colour in colours:
                open_ring(rings[colour][number + 2])
        for colour in colours:
            rings[colour][number].close()
            if number == 0:
                seconds[colour].far()
            elif number == 1:
                seconds[colour].raw_right_part()
            elif number == 2:
                seconds[colour].raw_left_part()
                seconds[colour].pass_right()
                seconds[colour].pass_left()
    for colour in colours:
        seconds[colour].close()
        open_ring(thirds[colour])
    for colour in colours:
        thirds[colour].pass_right()
        thirds[colour].pass_left()
    finals = []
    for colour in colours:
        thirds[colour].arrive()
        own = part(colour, {}, full)[...].astype(jnp.float32)
        last_left, last_right = thirds[colour].refs[2:4]
        finals.append(own + last_left[...].astype(jnp.float32) + last_right[...].astype(jnp.float32))
    return finals


def spread_kernel(
    tokens_ref, gain_ref, kv_ref, routes_attn_ref, routes_mlp_ref, wo_ref, wd_ref,
    out, wkv_out, routes_out, wo_out, wd_out,
    rows, routes, send, recv, local,
):
    place = Place()
    copies = Copies(send, recv)
    t, e, c, y = place.t, place.e, place.c, place.at["y"]
    others = [{"tok": (t + delta) % 16, "exp": e} for delta in range(1, 16)]
    across = [{"tok": t, "exp": (e + delta) % 8} for delta in range(1, 8)]
    values = tokens_ref[y].astype(jnp.float32)
    scale = lax.rsqrt(jnp.mean(values * values, axis=-1, keepdims=True) + epsilon)
    rows[...] = (values * scale * gain_ref[...]).astype(jnp.bfloat16)
    half = pl.ds(pl.multiple_of(c * HALF, HALF), HALF)
    own = pltpu.make_async_copy(
        rows.at[:, :, half],
        out.at[place.at["z"], place.at["x"], y, :, :, half],
        local.at[0],
    )
    own.start()
    routes[...] = jnp.zeros_like(routes)
    routes[0:2, 0:TOK_DEV] = routes_attn_ref[...].astype(jnp.float32)
    routes[2:4, 0:TOK_DEV] = routes_mlp_ref[...].astype(jnp.float32)
    greet(others + across)
    own.wait()
    own_routes = pltpu.make_async_copy(routes, routes_out.at[t], local.at[1])
    own_routes.start()
    side = Copies(send.at[pl.ds(GATHER_COPIES, 24)], recv.at[pl.ds(GATHER_COPIES, 24)])
    sibling = place.sibling()
    source = t // 2
    hops = (y + 4 - t // 4) % 4
    columns = pl.ds(pl.multiple_of((t % 2) * 256, 256), 256)
    mine = pl.ds(pl.multiple_of(c * HALF, HALF), HALF)
    theirs = pl.ds(pl.multiple_of((1 - c) * HALF, HALF), HALF)
    rising = pl.ds(pl.multiple_of(c * HALF, QUARTER), QUARTER)
    falling = pl.ds(pl.multiple_of(c * HALF + QUARTER, QUARTER), QUARTER)
    right = place.device(y=(y + 1) % 4)
    left = place.device(y=(y + 3) % 4)
    is_source = e == source

    def fan(number, lines, device, fresh=False):
        at = GATHER_COPIES + 24 + number
        return pltpu.make_async_remote_copy(
            src_ref=kv_ref.at[lines, columns] if fresh else wkv_out.at[lines, :],
            dst_ref=wkv_out.at[lines, :],
            send_sem=send.at[at],
            recv_sem=recv.at[at],
            device_id=device,
            device_id_type=MESH,
        )

    keep = pltpu.make_async_copy(kv_ref.at[mine, columns], wkv_out.at[mine, :], local.at[2])

    def first_hop():
        @pl.when(is_source)
        def _():
            fan(0, theirs, sibling, True).start()
            fan(1, rising, right, True).start()
            fan(2, falling, left, True).start()
            keep.start()

        for device in others:
            routed.append(side.start(routes, routes_out.at[t], device))
        routed.append(side.start(wo_ref.at[:, theirs], wo_out, sibling))
        for number in range(4):
            lanes = pl.ds(pl.multiple_of(number * 512 + (1 - c) * 256, 256), 256)
            target = wd_out.at[:, pl.ds(number * 256, 256)]
            routed.append(side.start(wd_ref.at[:, lanes], target, sibling))

    def second_hop():
        @pl.when((hops == 0) & jnp.logical_not(is_source))
        def _():
            fan(0, mine, sibling).wait_recv()
            fan(1, rising, right).start()
            fan(2, falling, left).start()

        @pl.when(hops == 1)
        def _():
            fan(1, rising, right).wait_recv()
            fan(1, rising, right).start()

        @pl.when(hops == 3)
        def _():
            fan(2, falling, left).wait_recv()
            fan(2, falling, left).start()

    def third_hop():
        @pl.when(hops == 2)
        def _():
            fan(1, rising, right).wait_recv()
            fan(1, rising, right).start()
            fan(2, falling, left).wait_recv()
            fan(2, falling, left).start()

    def last_hop():
        @pl.when(hops == 1)
        def _():
            fan(2, falling, left).wait_recv()

        @pl.when(hops == 3)
        def _():
            fan(1, rising, right).wait_recv()

        @pl.when(is_source)
        def _():
            keep.wait()

        shared.append(side.start(wkv_out.at[mine, :], wkv_out.at[mine, :], sibling))

    routed, shared = [], []
    torus_gather(place, copies, out, (first_hop, second_hop, third_hop, last_hop))
    shared[0].wait_recv()
    own_routes.wait()
    for copy in routed:
        copy.wait_recv()

    @pl.when(is_source)
    def _():
        fan(0, theirs, sibling, True).wait_send()

    @pl.when(hops != 3)
    def _():
        fan(1, rising, right).wait_send()

    @pl.when(hops != 1)
    def _():
        fan(2, falling, left).wait_send()

    copies.drain()
    side.drain()


def route_columns(routes_ref):
    eye = jnp.where(
        lax.broadcasted_iota(jnp.int32, (8, HD), 0) == lax.broadcasted_iota(jnp.int32, (8, HD), 1), 1.0, 0.0
    )
    parts = [
        lax.dot_general(
            routes_ref[number][:, :TOK_DEV], eye, (((0,), (0,)), ((), ())), preferred_element_type=jnp.float32
        )
        for number in range(2)
    ]
    return jnp.concatenate(parts, axis=0)


def pair_gate(first, second, expert, logits, base):
    chosen = (first == expert) | (second == expert)
    other = first + second - expert
    lane = lax.broadcasted_iota(jnp.int32, logits.shape, 1).astype(jnp.float32) - base
    own_logit = jnp.sum(jnp.where(lane == expert, logits, 0.0), axis=1, keepdims=True)
    other_logit = jnp.sum(jnp.where(lane == other, logits, 0.0), axis=1, keepdims=True)
    return chosen, jnp.where(chosen, 1.0 / (1.0 + jnp.exp(other_logit - own_logit)), 0.0)


PAGE_ROWS = PAGE + 16


def attend_kernel(
    lengths, table, x_ref, h1_ref, wq_ref, wkv_ref, router_ref, kv_ref, frequency_ref, routes_ref,
    out_ref, pages_ref,
    keys, values, weights, inner_cos, inner_sin, page_rows, page_sems,
):
    block = pl.program_id(0)
    tok = lax.axis_index("tok")
    expert = lax.axis_index("exp").astype(jnp.float32)
    second_start = lengths[0]
    third_start = lengths[0] + lengths[1]
    frequency = jnp.broadcast_to(frequency_ref[...], (8, HD))
    sign = jnp.where(lax.broadcasted_iota(jnp.int32, (1, HD), 1) < 64, -1.0, 1.0)

    def find(slot):
        def look(number, carry):
            begin, count, start = carry
            prompt, page = number // table.shape[1], number % table.shape[1]
            its_start = jnp.where(prompt == 0, 0, jnp.where(prompt == 1, second_start, third_start))
            remaining = lengths[prompt] - page * PAGE
            hit = (table[prompt, page, 0] == tok) & (table[prompt, page, 1] == slot) & (remaining > 0)
            return (
                jnp.where(hit, its_start + page * PAGE, begin),
                jnp.where(hit, jnp.minimum(remaining, PAGE), count),
                jnp.where(hit, its_start, start),
            )

        zero = jnp.int32(0)
        begin, count, start = lax.fori_loop(0, table.shape[0] * table.shape[1], look, (zero, zero, zero))
        aligned = jnp.minimum(begin // 16 * 16, TOKENS - PAGE_ROWS)
        return begin, count, start, pl.multiple_of(aligned, 16)

    def page_copy(slot, aligned):
        return pltpu.make_async_copy(
            h1_ref.at[pl.ds(aligned, PAGE_ROWS), :], page_rows.at[slot], page_sems.at[slot]
        )

    @pl.when(block == 0)
    def _():
        for slot in range(2):
            page_copy(slot, find(slot)[3]).start()
        weights[:, 0:HD] = wq_ref[...]
        weights[:, HD : 3 * HD] = wkv_ref[...]
        eye = jnp.where(
            lax.broadcasted_iota(jnp.int32, (8, HD), 0) == lax.broadcasted_iota(jnp.int32, (8, HD), 1), 1.0, 0.0
        )
        weights[:, 3 * HD :] = lax.dot_general(
            router_ref[...].astype(jnp.float32), eye, (((0,), (0,)), ((), ())), preferred_element_type=jnp.float32
        ).astype(jnp.bfloat16)
        angle = lax.broadcasted_iota(jnp.int32, (BLK, HD), 0).astype(jnp.float32) * frequency_ref[...]
        inner_cos[...] = jnp.cos(angle)
        inner_sin[...] = jnp.sin(angle)

    def outer(offset):
        angle = frequency * offset.astype(jnp.float32)
        return jnp.cos(angle)[0:1], jnp.sin(angle)[0:1]

    def turn(base_cos, base_sin, in_cos, in_sin):
        return base_cos * in_cos - base_sin * in_sin, (base_sin * in_cos + base_cos * in_sin) * sign

    row = lax.broadcasted_iota(jnp.int32, (BLK, 1), 0) + block * BLK
    in_second, in_third = row >= second_start, row >= third_start
    start = jnp.where(in_third, third_start, jnp.where(in_second, second_start, 0))
    bases = [outer(block * BLK - begin) for begin in (jnp.int32(0), second_start, third_start)]
    base_cos, base_sin = (
        jnp.where(in_third, bases[2][number], jnp.where(in_second, bases[1][number], bases[0][number]))
        for number in range(2)
    )
    cosine, sine = turn(base_cos, base_sin, inner_cos[...], inner_sin[...])

    def rotate(v):
        return (v * cosine + pltpu.roll(v, 64, 1) * sine).astype(jnp.bfloat16)

    projected = jnp.dot(x_ref[...], weights[...], preferred_element_type=jnp.float32)
    here = pl.ds(pl.multiple_of(block * BLK, BLK), BLK)
    keys[here, :] = rotate(projected[:, HD : 2 * HD])
    values[here, :] = projected[:, 2 * HD : 3 * HD].astype(jnp.bfloat16)
    queries = rotate(projected[:, :HD])
    columns = route_columns(routes_ref)
    chosen, gate = pair_gate(columns[:, 0:1], columns[:, 1:2], expert, projected[:, 3 * HD :], 0.0)
    row_number = lax.broadcasted_iota(jnp.int32, (BLK, BLK), 0)
    column_number = lax.broadcasted_iota(jnp.int32, (BLK, BLK), 1)
    below = jnp.where(row_number >= column_number, 1.0, 0.0).astype(jnp.bfloat16)
    flags = jnp.broadcast_to(jnp.where(chosen, 1.0, 0.0), (BLK, HD)).astype(jnp.bfloat16)
    rank = jnp.dot(below, flags, preferred_element_type=jnp.float32)[:, 0:1] - 1.0
    slot_number = lax.broadcasted_iota(jnp.int32, (BLK, SLOTS_BLK), 1).astype(jnp.float32)
    placing = jnp.where(chosen & (rank == slot_number), 1.0, 0.0).astype(jnp.bfloat16)
    lane = lax.broadcasted_iota(jnp.int32, (BLK, HD), 1)
    inside = lax.broadcasted_iota(jnp.int32, (BLK, HD), 0)
    digits = jnp.where(
        lane == 0,
        inside // 16,
        jnp.where(lane == 1, inside % 16, jnp.where(lane == 2, start // 64, jnp.where(lane == 3, start % 64, 0))),
    ).astype(jnp.float32).astype(jnp.bfloat16)
    taken = lax.dot_general(
        placing,
        jnp.concatenate([queries, digits], axis=1),
        (((0,), (0,)), ((), ())),
        preferred_element_type=jnp.float32,
    )
    picked = taken[:, :HD].astype(jnp.bfloat16)
    told = taken[:, HD:]
    highest_key = told[:, 0:1] * 16.0 + told[:, 1:2] + (block * BLK).astype(jnp.float32)
    lowest_key = told[:, 2:3] * 64.0 + told[:, 3:4]
    key_lane = lax.broadcasted_iota(jnp.int32, (SLOTS_BLK, BLK), 1)

    def visit(tile, carry):
        highest, denominator, summed = carry
        there = pl.ds(pl.multiple_of(tile * BLK, BLK), BLK)
        scores = lax.dot_general(
            picked, keys[there, :], (((1,), (1,)), ((), ())), preferred_element_type=jnp.float32
        ) * (HD**-0.5)
        number = (key_lane + tile * BLK).astype(jnp.float32)
        scores = jnp.where((number >= lowest_key) & (number <= highest_key), scores, -1e30)
        newest = jnp.maximum(highest, jnp.max(scores, axis=1, keepdims=True))
        shares = jnp.exp(scores - newest)
        shrink = jnp.exp(highest - newest)
        denominator = denominator * shrink + jnp.sum(shares, axis=1, keepdims=True)
        summed = summed * shrink + jnp.dot(
            shares.astype(jnp.bfloat16), values[there, :], preferred_element_type=jnp.float32
        )
        return newest, denominator, summed

    begin = block * BLK
    begin_of = jnp.where(begin >= third_start, third_start, jnp.where(begin >= second_start, second_start, 0))
    _, denominator, summed = lax.fori_loop(
        begin_of // BLK,
        block + 1,
        visit,
        (
            jnp.full((SLOTS_BLK, 1), -1e30, jnp.float32),
            jnp.zeros((SLOTS_BLK, 1), jnp.float32),
            jnp.zeros((SLOTS_BLK, HD), jnp.float32),
        ),
    )
    attended = (summed / denominator).astype(jnp.bfloat16)
    dense = jnp.dot(placing, attended, preferred_element_type=jnp.float32)
    out_ref[...] = (dense * gate).astype(jnp.bfloat16)

    @pl.when(block == pl.num_programs(0) - 1)
    def _():
        for slot in range(2):
            begin, count, start, aligned = find(slot)
            page_copy(slot, aligned).wait()
            part = jnp.dot(page_rows[slot], kv_ref[...], preferred_element_type=jnp.float32)
            page_cos, page_sin = turn(*outer(aligned - start), inner_cos[0:PAGE_ROWS], inner_sin[0:PAGE_ROWS])
            pieces = []
            for head in range(2):
                key = part[:, head * 256 : head * 256 + HD]
                pieces.append(key * page_cos + pltpu.roll(key, 64, 1) * page_sin)
                pieces.append(part[:, head * 256 + HD : (head + 1) * 256])
            run = jnp.concatenate(pieces, axis=1).astype(jnp.bfloat16)
            to = lax.broadcasted_iota(jnp.int32, (PAGE, PAGE_ROWS), 0)
            source = lax.broadcasted_iota(jnp.int32, (PAGE, PAGE_ROWS), 1)
            moving = jnp.where((source == to + (begin - aligned)) & (to < count), 1.0, 0.0).astype(jnp.bfloat16)
            pages_ref[slot] = jnp.dot(moving, run, preferred_element_type=jnp.float32).astype(jnp.bfloat16)


def middle_kernel(
    heads_ref, wo_ref, wo_pair_ref, tokens_ref, gain_ref,
    out, residual_out,
    paired, weights, held, shared, squares, rows, residual, send, recv, local, *buffers,
):
    place = Place()
    t, e, c, y = place.t, place.e, place.c, place.at["y"]
    across = [{"tok": t, "exp": (e + delta) % 8} for delta in range(1, 8)]
    around = [device for number, device in enumerate(place.neighbours()) if number in (1, 2, 3, 4)]
    greet(around + across)
    copies = Copies(send, recv)
    sibling = place.sibling()
    half = pl.ds(pl.multiple_of(c * HALF, HALF), HALF)
    given = copies.start(heads_ref, paired, sibling)
    weights[0:HD, :] = wo_ref[:, half]
    weights[HD : 2 * HD, :] = wo_pair_ref[...]
    given.wait_recv()

    def project(number, carry):
        lines = pl.ds(pl.multiple_of(number * TOK_DEV, TOK_DEV), TOK_DEV)
        both = jnp.concatenate([heads_ref[lines, :], paired[lines, :]], axis=1)
        part = jnp.dot(both, weights[...], preferred_element_type=jnp.float32)
        held[number // 4, number % 4] = part.astype(jnp.bfloat16).reshape(4, 3, 16, HALF)
        return carry

    lax.fori_loop(0, 16, project, 0)
    sums = torus_sum(place, copies, held, buffers)
    square = []
    for colour in range(3):
        value = tokens_ref[y, colour, :, half].astype(jnp.float32) + sums[colour]
        residual[colour] = value
        square.append(jnp.sum(value * value, axis=-1, keepdims=True))
        shared[colour] = jnp.broadcast_to(square[colour], (16, HD))
    swapped = copies.start(shared, squares, sibling)
    for colour in range(3):
        for number in range(4):
            rows_here = pl.ds(colour * 16, 16)
            residual_out_part = residual[colour, :, number * 256 : (number + 1) * 256]
            buffers[-1][number, rows_here, :] = residual_out_part
    pieces = buffers[-1]
    base = send.shape[0] - 4

    def piece(number, sender):
        return pltpu.make_async_remote_copy(
            src_ref=pieces.at[number],
            dst_ref=residual_out.at[sender],
            send_sem=send.at[base + number],
            recv_sem=recv.at[base + sender],
            device_id={"tok": t, "exp": 4 * c + number},
            device_id_type=MESH,
        )

    for number in range(4):

        @pl.when(4 * c + number == e)
        def _():
            keep = pltpu.make_async_copy(pieces.at[number], residual_out.at[y], local.at[1])
            keep.start()
            keep.wait()

        @pl.when(4 * c + number != e)
        def _():
            piece(number, y).start()

    swapped.wait_recv()
    for colour in range(3):
        total = square[colour] + squares[colour][:, 0:1]
        scale = lax.rsqrt(total * (1.0 / D) + epsilon)
        rows[colour] = (residual[colour] * scale * gain_ref[:, half]).astype(jnp.bfloat16)
    own = pltpu.make_async_copy(
        rows, out.at[place.at["z"], place.at["x"], y, :, :, half], local.at[0]
    )
    own.start()
    own.wait()
    torus_gather(place, copies, out)
    for sender in range(4):
        itself = (y == sender) & (c == e // 4)

        @pl.when(jnp.logical_not(itself))
        def _():
            piece(0, sender).wait_recv()

    for number in range(4):

        @pl.when(4 * c + number != e)
        def _():
            piece(number, y).wait_send()

    copies.drain()


def hidden_kernel(x_ref, wg_ref, wu_ref, router_ref, routes_ref, out_ref, weights):
    expert = lax.axis_index("exp").astype(jnp.float32)

    @pl.when(pl.program_id(0) == 0)
    def _():
        weights[0:FF_DEV, :] = wg_ref[...]
        weights[FF_DEV:BLK, :] = jnp.zeros((BLK - FF_DEV, D), jnp.bfloat16)
        weights[BLK : BLK + FF_DEV, :] = wu_ref[...]
        weights[BLK + FF_DEV :, :] = jnp.zeros((BLK - FF_DEV, D), jnp.bfloat16)
        router = jnp.concatenate([router_ref[...].astype(jnp.float32), jnp.zeros((8, D), jnp.float32)], axis=0)
        weights[BLK + FF_DEV : BLK + FF_DEV + 16, :] = router.astype(jnp.bfloat16)

    both = lax.dot_general(
        x_ref[...], weights[...], (((1,), (1,)), ((), ())), preferred_element_type=jnp.float32
    )
    columns = route_columns(routes_ref)
    _, gate = pair_gate(columns[:, 2:3], columns[:, 3:4], expert, both[:, 5 * HD :], float(FF_DEV - 2 * HD))
    opened, upward = both[:, :FF_DEV], both[:, BLK : BLK + FF_DEV]
    hidden = opened / (1.0 + jnp.exp(-opened)) * upward
    out_ref[...] = (hidden * gate).astype(jnp.bfloat16)


def last_kernel(
    hidden_ref, wd_ref, wd_pair_ref, residual_ref,
    out_ref,
    paired, held, send, recv, *buffers,
):
    place = Place()
    c = place.c
    greet(place.neighbours())
    copies = Copies(send, recv)
    given = copies.start(hidden_ref, paired, place.sibling())
    given.wait_recv()

    def project(number, carry):
        lines = pl.ds(pl.multiple_of(number * TOK_DEV, TOK_DEV), TOK_DEV)
        own, pair = hidden_ref[lines, :], paired[lines, :]
        for at in range(4):
            lanes = pl.ds(pl.multiple_of(at * 512 + c * 256, 256), 256)
            part = jnp.dot(own, wd_ref[:, lanes], preferred_element_type=jnp.float32)
            part += jnp.dot(
                pair, wd_pair_ref[:, at * 256 : (at + 1) * 256], preferred_element_type=jnp.float32
            )
            held[number // 4, number % 4, at] = part.astype(jnp.bfloat16).reshape(3, 64, 256)
        return carry

    lax.fori_loop(0, 16, project, 0)
    sums = torus_sum(place, copies, held, buffers)
    for colour in range(3):
        lines = slice(colour * 64, (colour + 1) * 64)
        out_ref[lines, :] = (residual_ref[lines, :] + sums[colour]).astype(jnp.bfloat16)
    copies.drain()


def shards(
    tokens,
    gain_attn,
    router_attn,
    kv_weight,
    query_weight,
    out_weight,
    gain_mlp,
    router_mlp,
    gate_weight,
    up_weight,
    down_weight,
    routes_attn,
    routes_mlp,
    lengths,
    page_table,
):
    bf16 = jnp.bfloat16
    struct = jax.ShapeDtypeStruct
    tokens_parts = tokens.reshape(4, 3, 16, D)
    spread_count = GATHER_COPIES + 24 + 3
    gathered, wkv, routes, wo_pair, wd_pair = pl.pallas_call(
        spread_kernel,
        out_shape=(
            struct((4, 4, 4, 3, 16, D), bf16),
            struct((D, 256), bf16),
            struct((16, 8, 256), jnp.float32),
            struct((HD, HALF), bf16),
            struct((FF_DEV, HALF), bf16),
        ),
        in_specs=[VMEM, VMEM, ANY, VMEM, VMEM, ANY, ANY],
        out_specs=(ANY,) * 5,
        scratch_shapes=[
            pltpu.VMEM((3, 16, D), bf16),
            pltpu.VMEM((8, 256), jnp.float32),
            pltpu.SemaphoreType.DMA((spread_count,)),
            pltpu.SemaphoreType.DMA((spread_count,)),
            pltpu.SemaphoreType.DMA((3,)),
        ],
        compiler_params=pltpu.CompilerParams(collective_id=0, has_side_effects=True),
        name="spread",
    )(
        tokens_parts, gain_attn.reshape(1, 1, D), kv_weight, routes_attn.T, routes_mlp.T, out_weight[0], down_weight[0]
    )
    h1 = gathered.reshape(TOKENS, D)
    frequency = (10000.0 ** -(np.arange(HD) % 64 * (2.0 / HD))).astype(np.float32).reshape(1, HD)
    steps = TOKENS // BLK

    def whole(*shape):
        return pl.BlockSpec(shape, lambda i, *_: (0,) * len(shape))

    def lines(width):
        return pl.BlockSpec((BLK, width), lambda i, *_: (i, 0))

    routes_spec = pl.BlockSpec((2, 8, 256), lambda i, *_: (i, 0, 0))
    heads, kv_pages = pl.pallas_call(
        attend_kernel,
        out_shape=(struct((TOKENS, HD), bf16), struct((2, PAGE, 512), bf16)),
        grid_spec=pltpu.PrefetchScalarGridSpec(
            num_scalar_prefetch=2,
            grid=(steps,),
            in_specs=[
                lines(D), ANY, whole(D, HD), whole(D, 256), whole(8, D), whole(D, 512), whole(1, HD), routes_spec,
            ],
            out_specs=(lines(HD), whole(2, PAGE, 512)),
            scratch_shapes=[
                pltpu.VMEM((TOKENS, HD), bf16),
                pltpu.VMEM((TOKENS, HD), bf16),
                pltpu.VMEM((D, 4 * HD), bf16),
                pltpu.VMEM((BLK, HD), jnp.float32),
                pltpu.VMEM((BLK, HD), jnp.float32),
                pltpu.VMEM((2, PAGE_ROWS, D), bf16),
                pltpu.SemaphoreType.DMA((2,)),
            ],
        ),
        name="attend",
    )(lengths, page_table, h1, h1, query_weight[0], wkv, router_attn.T, kv_weight, jnp.asarray(frequency), routes)

    middle_count = 2 + SUM_COPIES + GATHER_COPIES + 4
    gathered, residual = pl.pallas_call(
        middle_kernel,
        out_shape=(struct((4, 4, 4, 3, 16, D), bf16), struct((4, 48, 256), jnp.float32)),
        in_specs=[VMEM] * 5,
        out_specs=(ANY, ANY),
        scratch_shapes=[
            pltpu.VMEM((TOKENS, HD), bf16),
            pltpu.VMEM((2 * HD, HALF), bf16),
            pltpu.VMEM((4, 4, 4, 3, 16, HALF), bf16),
            pltpu.VMEM((3, 16, HD), jnp.float32),
            pltpu.VMEM((3, 16, HD), jnp.float32),
            pltpu.VMEM((3, 16, HALF), bf16),
            pltpu.VMEM((3, 16, HALF), jnp.float32),
            pltpu.SemaphoreType.DMA((middle_count,)),
            pltpu.SemaphoreType.DMA((middle_count,)),
            pltpu.SemaphoreType.DMA((2,)),
            *sum_buffers(16, HALF),
            pltpu.VMEM((4, 48, 256), jnp.float32),
        ],
        compiler_params=pltpu.CompilerParams(collective_id=1, has_side_effects=True),
        name="middle",
    )(heads, out_weight[0], wo_pair, tokens_parts, gain_mlp.reshape(1, D))
    h2 = gathered.reshape(TOKENS, D)

    hidden = pl.pallas_call(
        hidden_kernel,
        out_shape=struct((TOKENS, FF_DEV), bf16),
        grid_spec=pltpu.PrefetchScalarGridSpec(
            num_scalar_prefetch=0,
            grid=(steps,),
            in_specs=[lines(D), whole(FF_DEV, D), whole(FF_DEV, D), whole(8, D), routes_spec],
            out_specs=lines(FF_DEV),
            scratch_shapes=[pltpu.VMEM((2 * BLK, D), bf16)],
        ),
        name="hidden",
    )(h2, gate_weight[0].T, up_weight[0].T, router_mlp.T, routes)

    last_count = 1 + SUM_COPIES
    mixed = pl.pallas_call(
        last_kernel,
        out_shape=struct((TOK_DEV, 256), bf16),
        in_specs=[VMEM] * 4,
        out_specs=VMEM,
        scratch_shapes=[
            pltpu.VMEM((TOKENS, FF_DEV), bf16),
            pltpu.VMEM((4, 4, 4, 3, 64, 256), bf16),
            pltpu.SemaphoreType.DMA((last_count,)),
            pltpu.SemaphoreType.DMA((last_count,)),
            *sum_buffers(64, 256),
        ],
        compiler_params=pltpu.CompilerParams(collective_id=2, has_side_effects=True),
        name="last",
    )(hidden, down_weight[0], wd_pair, residual.reshape(TOK_DEV, 256))
    return (mixed, kv_pages)


def solution(mesh):
    return jax.shard_map(
        shards,
        mesh=mesh,
        in_specs=(
            P("tok", None),
            P(),
            P(),
            P(None, "exp"),
            P("exp", None, "tok"),
            P("exp", "tok", None),
            P(),
            P(),
            P("exp", None, "tok"),
            P("exp", None, "tok"),
            P("exp", "tok", None),
            P("tok", None),
            P("tok", None),
            P(),
            P(),
        ),
        out_specs=(P("tok", "exp"), P("tok", None, "exp")),
        check_vma=False,
    )
```

time: 324 us -> 259 us (0.80)
  other arithmetic: 27.6 us -> 0 us
  Pallas kernels: 273 us -> 255 us
  local copies, waits for them, and re-layouts: 20.5 us -> 2.93 us
    pallas_call x1, Pallas kernels: 73.5 us -> 50.9 us  [shards(): pl.pallas_call(spread_kernel, out_shape=(struct((4, 4, 4, 3, 16, D), bf16...]
    gather x1 -> x0, local copies, waits for them, and re-layouts: 8.7 us -> none  [shards(): jnp.take(h1, jnp.concatenate(page_rows), axis=0, mode='clip')]
    neg x1 -> x0, other arithmetic: 5.99 us -> none  [shards(): sin_table = jnp.concatenate([-sine, sine], axis=1)]
    concatenate x7 -> x0, other arithmetic: 5.46 us -> none  [the longest x1 1.67 us: shards(): sin_table = jnp.concatenate([-sine, sine], axis=1)]
    pallas_call x1, Pallas kernels: 34.5 us -> 39.7 us  [shards(): pl.pallas_call(attend_kernel, out_shape=(struct((TOKENS, HD), bf16), stru...]
where the time goes in v2:
time: 259 us; the launch traced here: 258 us
  Pallas kernels  255 us (98%)
  local copies, waits for them, and re-layouts  2.93 us (1%)
    pallas_call x1, Pallas kernels, shards(): pl.pallas_call(middle_kernel, out_shape=(struct((4, 4, 4, 3, 16, D), bf16...  88.6 us
    pallas_call x1, Pallas kernels, shards(): pl.pallas_call(last_kernel, out_shape=struct((TOK_DEV, 256), bf16), in_sp...  55 us
    pallas_call x1, Pallas kernels, shards(): pl.pallas_call(spread_kernel, out_shape=(struct((4, 4, 4, 3, 16, D), bf16...  50.9 us
    pallas_call x1, Pallas kernels, shards(): pl.pallas_call(attend_kernel, out_shape=(struct((TOKENS, HD), bf16), stru...  39.7 us
    pallas_call x1, Pallas kernels, shards(): pl.pallas_call(hidden_kernel, out_shape=struct((TOKENS, FF_DEV), bf16), g...  20.6 us

profile of v2, /device:TPU:0, one launch (start us, length us, event | category | flops | bytes accessed | tf_op | source)
XLA Modules:
  0.0 258.3 jit_solution(4555233529531287085)
XLA Ops:
  0.6 1.4 copy.18.table
  2.0 50.9 %spread.1 = (bf16[4,4,4,3,16,2048]{5,4,3,2,1,0:T(8,128)(2,1)}, bf16[2048,256]{1,0:T(8,128)(2,1)}, f32[16,8,256]{2,1,0:T(8,128)}, bf16[128,1024]{1,0:T(8,128)(2,1)}, bf16[352,1024]{1,0:T(8,128)(2,1)}) custom-call(bf16[4,3,16,2048]{3,2,1,0:T(8,128)(2,1)} %bitcast.24, f32[1,1,2048]{2,1,0:T(1,128)} %bitcast.34, bf16[2048,512]{1,0:T(8,128)(2,1)} %kv_ref.3, ...), custom_call_target="tpu_custom_call" | custom-call | tf_op jit(solution)/shard_map/spread/pallas_call | solution.py:826
  52.9 39.7 %attend.1 = (bf16[3072,128]{1,0:T(8,128)(2,1)}, bf16[2,128,512]{2,1,0:T(8,128)(2,1)}) custom-call(s32[3]{0:T(128)} %lengths.1, s32[3,12,2]{2,1,0:T(8,128)} %copy.18.table, bf16[3072,2048]{1,0:T(8,128)(2,1)} %bitcast.19, bf16[3072,2048]{1,0:T(8,128)(2,1)} %bitcast.20, bf16[2048,128]{1,0:T(8,128)(2,1)} %bitcast.30, ...), custom_call_target="tpu_custom_call" | custom-call | tf_op jit(solution)/shard_map/attend/pallas_call | solution.py:860
  92.6 88.6 %middle.1 = (bf16[4,4,4,3,16,2048]{5,4,3,2,1,0:T(8,128)(2,1)}, f32[4,48,256]{2,1,0:T(8,128)}) custom-call(bf16[3072,128]{1,0:T(8,128)(2,1)} %get-tuple-element.14.heads_ref, bf16[128,2048]{1,0:T(8,128)(2,1)} %bitcast.27, bf16[128,1024]{1,0:T(8,128)(2,1)} %get-tuple-element.15.wo_pair_ref, bf16[4,3,16,2048]{3,2,1,0:T(8,128)(2,1)} %bitcast.25, f32[1,2048]{1,0:T(1,128)} %bitcast.35), custom_call_target="tpu_custom_call" | custom-call | tf_op jit(solution)/shard_map/middle/pallas_call | solution.py:884
  181.2 20.6 %hidden.1.hidden_ref = bf16[3072,352]{1,0:T(8,128)(2,1)} custom-call(bf16[3072,2048]{1,0:T(8,128)(2,1)} %bitcast.21, bf16[352,2048]{1,0:T(8,128)(2,1)} %bitcast.28, bf16[352,2048]{1,0:T(8,128)(2,1)} %bitcast.29, bf16[8,2048]{1,0:T(8,128)(2,1)} %bitcast.32, f32[16,8,256]{2,1,0:T(8,128)} %get-tuple-element.13.routes_ref), custom_call_target="tpu_custom_call" | custom-call | tf_op jit(solution)/shard_map/hidden/pallas_call | solution.py:908
  201.8 55.0 %last.1 = bf16[192,256]{1,0:T(8,128)(2,1)} custom-call(bf16[3072,352]{1,0:T(8,128)(2,1)} %hidden.1.hidden_ref, bf16[352,2048]{1,0:T(8,128)(2,1)} %bitcast.23, bf16[352,1024]{1,0:T(8,128)(2,1)} %get-tuple-element.17.wd_pair_ref, f32[192,256]{1,0:T(8,128)} %bitcast.31), custom_call_target="tpu_custom_call" | custom-call | tf_op jit(solution)/shard_map/last/pallas_call | solution.py:922
  256.8 1.5 copy.20

commit v3 on v2

--- a/solution.py
+++ b/solution.py
@@ -219,7 +219,15 @@
 SUM_COPIES = 3 * 36
 
 
-def torus_sum(place, copies, held, buffers):
+def exchange(place, copies, mine, theirs):
+    given = {}
+    for delta in (2, 1, 3, 0):
+        lines = pl.ds(pl.multiple_of(place.step("z", delta) * 4 * TOK_DEV, TOK_DEV), 4 * TOK_DEV)
+        given[delta] = copies.start(mine.at[lines, :], theirs.at[lines, :], place.sibling())
+    return given
+
+
+def torus_sum(place, copies, held, buffers, produce):
     width = held.shape[-1]
     first, second, full = pl.ds(0, width // 2), pl.ds(width // 2, width // 2), slice(None)
     colours = range(3)
@@ -308,8 +316,18 @@
         ring.raw_right_part()
         ring.raw_left_part()
 
+    produce(2)
     for number in range(2):
-        for colour in colours:
+        rings[2][number].far()
+    produce(1)
+    for number in range(2):
+        rings[2][number].raw_right_part()
+    produce(3)
+    for number in range(2):
+        rings[2][number].raw_left_part()
+    produce(0)
+    for number in range(2):
+        for colour in range(2):
             open_ring(rings[colour][number])
     for number in range(4):
         for colour in colours:
@@ -344,11 +362,17 @@
 
 
 def spread_kernel(
-    tokens_ref, gain_ref, kv_ref, routes_attn_ref, routes_mlp_ref, wo_ref, wd_ref,
-    out, wkv_out, routes_out, wo_out, wd_out,
-    rows, routes, send, recv, local,
+    tokens_ref, gain_ref, kv_ref, routes_attn_ref, routes_mlp_ref, wo_ref, wd_ref, wg_ref, wu_ref, router_ref,
+    out, wkv_out, routes_out, wo_out, wd_out, both_out,
+    rows, routes, opened, upward, both, send, recv, local,
 ):
     place = Place()
+    fetches = [
+        pltpu.make_async_copy(wg_ref, opened, local.at[3]),
+        pltpu.make_async_copy(wu_ref, upward, local.at[4]),
+    ]
+    for fetch in fetches:
+        fetch.start()
     copies = Copies(send, recv)
     t, e, c, y = place.t, place.e, place.c, place.at["y"]
     others = [{"tok": (t + delta) % 16, "exp": e} for delta in range(1, 16)]
@@ -452,8 +476,51 @@
 
         shared.append(side.start(wkv_out.at[mine, :], wkv_out.at[mine, :], sibling))
 
+    def turned(ref, shift, width):
+        eye = jnp.where(
+            lax.broadcasted_iota(jnp.int32, (ref.shape[0], width), 0) + shift
+            == lax.broadcasted_iota(jnp.int32, (ref.shape[0], width), 1),
+            1.0,
+            0.0,
+        ).astype(jnp.bfloat16)
+
+        def some(at):
+            return lax.dot_general(
+                ref[:, at], eye, (((0,), (0,)), ((), ())), preferred_element_type=jnp.float32
+            ).astype(jnp.bfloat16)
+
+        return some
+
+    def turn_gate():
+        fetches[0].wait()
+        some = turned(opened, 0, BLK)
+        for number in range(4):
+            at = slice(number * 512, (number + 1) * 512)
+            both[at, 0:BLK] = some(at)
+
+    def turn_up():
+        fetches[1].wait()
+        some = turned(upward, 0, BLK)
+        routing = turned(router_ref, FF_DEV - 2 * HD, HD)
+        for number in range(4):
+            at = slice(number * 512, (number + 1) * 512)
+            both[at, BLK : 2 * BLK] = some(at)
+            both[at, BLK + 2 * HD : 2 * BLK] += routing(at)
+        stored.start()
+
+    stored = pltpu.make_async_copy(both, both_out, local.at[5])
+
+    def second_step():
+        second_hop()
+        turn_gate()
+
+    def third_step():
+        third_hop()
+        turn_up()
+
     routed, shared = [], []
-    torus_gather(place, copies, out, (first_hop, second_hop, third_hop, last_hop))
+    torus_gather(place, copies, out, (first_hop, second_step, third_step, last_hop))
+    stored.wait()
     shared[0].wait_recv()
     own_routes.wait()
     for copy in routed:
@@ -516,10 +583,10 @@
     def find(slot):
         def look(number, carry):
             begin, count, start = carry
-            prompt, page = number // table.shape[1], number % table.shape[1]
+            prompt, page = number // table.shape[2], number % table.shape[2]
             its_start = jnp.where(prompt == 0, 0, jnp.where(prompt == 1, second_start, third_start))
             remaining = lengths[prompt] - page * PAGE
-            hit = (table[prompt, page, 0] == tok) & (table[prompt, page, 1] == slot) & (remaining > 0)
+            hit = (table[prompt, 0, page] == tok) & (table[prompt, 1, page] == slot) & (remaining > 0)
             return (
                 jnp.where(hit, its_start + page * PAGE, begin),
                 jnp.where(hit, jnp.minimum(remaining, PAGE), count),
@@ -527,7 +594,7 @@
             )
 
         zero = jnp.int32(0)
-        begin, count, start = lax.fori_loop(0, table.shape[0] * table.shape[1], look, (zero, zero, zero))
+        begin, count, start = lax.fori_loop(0, table.shape[0] * table.shape[2], look, (zero, zero, zero))
         aligned = jnp.minimum(begin // 16 * 16, TOKENS - PAGE_ROWS)
         return begin, count, start, pl.multiple_of(aligned, 16)
 
@@ -590,8 +657,8 @@
     inside = lax.broadcasted_iota(jnp.int32, (BLK, HD), 0)
     digits = jnp.where(
         lane == 0,
-        inside // 16,
-        jnp.where(lane == 1, inside % 16, jnp.where(lane == 2, start // 64, jnp.where(lane == 3, start % 64, 0))),
+        inside >> 4,
+        jnp.where(lane == 1, inside & 15, jnp.where(lane == 2, start >> 6, jnp.where(lane == 3, start & 63, 0))),
     ).astype(jnp.float32).astype(jnp.bfloat16)
     taken = lax.dot_general(
         placing,
@@ -670,20 +737,24 @@
     copies = Copies(send, recv)
     sibling = place.sibling()
     half = pl.ds(pl.multiple_of(c * HALF, HALF), HALF)
-    given = copies.start(heads_ref, paired, sibling)
+    given = exchange(place, copies, heads_ref, paired)
     weights[0:HD, :] = wo_ref[:, half]
     weights[HD : 2 * HD, :] = wo_pair_ref[...]
-    given.wait_recv()
-
-    def project(number, carry):
-        lines = pl.ds(pl.multiple_of(number * TOK_DEV, TOK_DEV), TOK_DEV)
-        both = jnp.concatenate([heads_ref[lines, :], paired[lines, :]], axis=1)
-        part = jnp.dot(both, weights[...], preferred_element_type=jnp.float32)
-        held[number // 4, number % 4] = part.astype(jnp.bfloat16).reshape(4, 3, 16, HALF)
-        return carry
-
-    lax.fori_loop(0, 16, project, 0)
-    sums = torus_sum(place, copies, held, buffers)
+
+    def produce(delta):
+        given[delta].wait_recv()
+        z = place.step("z", delta)
+
+        def project(x, carry):
+            lines = pl.ds(pl.multiple_of((z * 4 + x) * TOK_DEV, TOK_DEV), TOK_DEV)
+            both = jnp.concatenate([heads_ref[lines, :], paired[lines, :]], axis=1)
+            part = jnp.dot(both, weights[...], preferred_element_type=jnp.float32)
+            held[z, x] = part.astype(jnp.bfloat16).reshape(4, 3, 16, HALF)
+            return carry
+
+        lax.fori_loop(0, 4, project, 0)
+
+    sums = torus_sum(place, copies, held, buffers, produce)
     square = []
     for colour in range(3):
         value = tokens_ref[y, colour, :, half].astype(jnp.float32) + sums[colour]
@@ -748,21 +819,9 @@
     copies.drain()
 
 
-def hidden_kernel(x_ref, wg_ref, wu_ref, router_ref, routes_ref, out_ref, weights):
+def hidden_kernel(x_ref, weights_ref, routes_ref, out_ref):
     expert = lax.axis_index("exp").astype(jnp.float32)
-
-    @pl.when(pl.program_id(0) == 0)
-    def _():
-        weights[0:FF_DEV, :] = wg_ref[...]
-        weights[FF_DEV:BLK, :] = jnp.zeros((BLK - FF_DEV, D), jnp.bfloat16)
-        weights[BLK : BLK + FF_DEV, :] = wu_ref[...]
-        weights[BLK + FF_DEV :, :] = jnp.zeros((BLK - FF_DEV, D), jnp.bfloat16)
-        router = jnp.concatenate([router_ref[...].astype(jnp.float32), jnp.zeros((8, D), jnp.float32)], axis=0)
-        weights[BLK + FF_DEV : BLK + FF_DEV + 16, :] = router.astype(jnp.bfloat16)
-
-    both = lax.dot_general(
-        x_ref[...], weights[...], (((1,), (1,)), ((), ())), preferred_element_type=jnp.float32
-    )
+    both = jnp.dot(x_ref[...], weights_ref[...], preferred_element_type=jnp.float32)
     columns = route_columns(routes_ref)
     _, gate = pair_gate(columns[:, 2:3], columns[:, 3:4], expert, both[:, 5 * HD :], float(FF_DEV - 2 * HD))
     opened, upward = both[:, :FF_DEV], both[:, BLK : BLK + FF_DEV]
@@ -779,23 +838,27 @@
     c = place.c
     greet(place.neighbours())
     copies = Copies(send, recv)
-    given = copies.start(hidden_ref, paired, place.sibling())
-    given.wait_recv()
-
-    def project(number, carry):
-        lines = pl.ds(pl.multiple_of(number * TOK_DEV, TOK_DEV), TOK_DEV)
-        own, pair = hidden_ref[lines, :], paired[lines, :]
-        for at in range(4):
-            lanes = pl.ds(pl.multiple_of(at * 512 + c * 256, 256), 256)
-            part = jnp.dot(own, wd_ref[:, lanes], preferred_element_type=jnp.float32)
-            part += jnp.dot(
-                pair, wd_pair_ref[:, at * 256 : (at + 1) * 256], preferred_element_type=jnp.float32
-            )
-            held[number // 4, number % 4, at] = part.astype(jnp.bfloat16).reshape(3, 64, 256)
-        return carry
-
-    lax.fori_loop(0, 16, project, 0)
-    sums = torus_sum(place, copies, held, buffers)
+    given = exchange(place, copies, hidden_ref, paired)
+
+    def produce(delta):
+        given[delta].wait_recv()
+        z = place.step("z", delta)
+
+        def project(x, carry):
+            lines = pl.ds(pl.multiple_of((z * 4 + x) * TOK_DEV, TOK_DEV), TOK_DEV)
+            own, pair = hidden_ref[lines, :], paired[lines, :]
+            for at in range(4):
+                lanes = pl.ds(pl.multiple_of(at * 512 + c * 256, 256), 256)
+                part = jnp.dot(own, wd_ref[:, lanes], preferred_element_type=jnp.float32)
+                part += jnp.dot(
+                    pair, wd_pair_ref[:, at * 256 : (at + 1) * 256], preferred_element_type=jnp.float32
+                )
+                held[z, x, at] = part.astype(jnp.bfloat16).reshape(3, 64, 256)
+            return carry
+
+        lax.fori_loop(0, 4, project, 0)
+
+    sums = torus_sum(place, copies, held, buffers, produce)
     for colour in range(3):
         lines = slice(colour * 64, (colour + 1) * 64)
         out_ref[lines, :] = (residual_ref[lines, :] + sums[colour]).astype(jnp.bfloat16)
@@ -823,7 +886,7 @@
     struct = jax.ShapeDtypeStruct
     tokens_parts = tokens.reshape(4, 3, 16, D)
     spread_count = GATHER_COPIES + 24 + 3
-    gathered, wkv, routes, wo_pair, wd_pair = pl.pallas_call(
+    gathered, wkv, routes, wo_pair, wd_pair, both = pl.pallas_call(
         spread_kernel,
         out_shape=(
             struct((4, 4, 4, 3, 16, D), bf16),
@@ -831,20 +894,25 @@
             struct((16, 8, 256), jnp.float32),
             struct((HD, HALF), bf16),
             struct((FF_DEV, HALF), bf16),
+            struct((D, 2 * BLK), bf16),
         ),
-        in_specs=[VMEM, VMEM, ANY, VMEM, VMEM, ANY, ANY],
-        out_specs=(ANY,) * 5,
+        in_specs=[VMEM, VMEM, ANY, VMEM, VMEM, ANY, ANY, ANY, ANY, VMEM],
+        out_specs=(ANY,) * 6,
         scratch_shapes=[
             pltpu.VMEM((3, 16, D), bf16),
             pltpu.VMEM((8, 256), jnp.float32),
+            pltpu.VMEM((FF_DEV, D), bf16),
+            pltpu.VMEM((FF_DEV, D), bf16),
+            pltpu.VMEM((D, 2 * BLK), bf16),
             pltpu.SemaphoreType.DMA((spread_count,)),
             pltpu.SemaphoreType.DMA((spread_count,)),
-            pltpu.SemaphoreType.DMA((3,)),
+            pltpu.SemaphoreType.DMA((6,)),
         ],
         compiler_params=pltpu.CompilerParams(collective_id=0, has_side_effects=True),
         name="spread",
     )(
-        tokens_parts, gain_attn.reshape(1, 1, D), kv_weight, routes_attn.T, routes_mlp.T, out_weight[0], down_weight[0]
+        tokens_parts, gain_attn.reshape(1, 1, D), kv_weight, routes_attn.T, routes_mlp.T, out_weight[0], down_weight[0],
+        gate_weight[0].T, up_weight[0].T, router_mlp.T,
     )
     h1 = gathered.reshape(TOKENS, D)
     frequency = (10000.0 ** -(np.arange(HD) % 64 * (2.0 / HD))).astype(np.float32).reshape(1, HD)
@@ -878,9 +946,9 @@
             ],
         ),
         name="attend",
-    )(lengths, page_table, h1, h1, query_weight[0], wkv, router_attn.T, kv_weight, jnp.asarray(frequency), routes)
-
-    middle_count = 2 + SUM_COPIES + GATHER_COPIES + 4
+    )(lengths, jnp.swapaxes(page_table, 1, 2), h1, h1, query_weight[0], wkv, router_attn.T, kv_weight, jnp.asarray(frequency), routes)
+
+    middle_count = 5 + SUM_COPIES + GATHER_COPIES + 4
     gathered, residual = pl.pallas_call(
         middle_kernel,
         out_shape=(struct((4, 4, 4, 3, 16, D), bf16), struct((4, 48, 256), jnp.float32)),
@@ -911,14 +979,13 @@
         grid_spec=pltpu.PrefetchScalarGridSpec(
             num_scalar_prefetch=0,
             grid=(steps,),
-            in_specs=[lines(D), whole(FF_DEV, D), whole(FF_DEV, D), whole(8, D), routes_spec],
+            in_specs=[lines(D), whole(D, 2 * BLK), routes_spec],
             out_specs=lines(FF_DEV),
-            scratch_shapes=[pltpu.VMEM((2 * BLK, D), bf16)],
         ),
         name="hidden",
-    )(h2, gate_weight[0].T, up_weight[0].T, router_mlp.T, routes)
-
-    last_count = 1 + SUM_COPIES
+    )(h2, both, routes)
+
+    last_count = 4 + SUM_COPIES
     mixed = pl.pallas_call(
         last_kernel,
         out_shape=struct((TOK_DEV, 256), bf16),

time: 259 us -> 255 us (0.985)
  Pallas kernels: 255 us -> 252 us
    pallas_call x1, Pallas kernels: 55 us -> 52.3 us  [shards(): pl.pallas_call(last_kernel, out_shape=struct((TOK_DEV, 256), bf16), in_sp...]
where the time goes in v3:
time: 255 us; the launch traced here: 254 us
  Pallas kernels  252 us (99%)
    pallas_call x1, Pallas kernels, shards(): pl.pallas_call(middle_kernel, out_shape=(struct((4, 4, 4, 3, 16, D), bf16...  87.1 us
    pallas_call x1, Pallas kernels, shards(): pl.pallas_call(last_kernel, out_shape=struct((TOK_DEV, 256), bf16), in_sp...  52.3 us
    pallas_call x1, Pallas kernels, shards(): pl.pallas_call(spread_kernel, out_shape=(struct((4, 4, 4, 3, 16, D), bf16...  52 us
    pallas_call x1, Pallas kernels, shards(): pl.pallas_call(attend_kernel, out_shape=(struct((TOKENS, HD), bf16), stru...  40.3 us
    pallas_call x1, Pallas kernels, shards(): pl.pallas_call(hidden_kernel, out_shape=struct((TOKENS, FF_DEV), bf16), g...  20.6 us

profile of v3, /device:TPU:0, one launch (start us, length us, event | category | flops | bytes accessed | tf_op | source)
XLA Modules:
  0.0 254.4 jit_solution(5240209345135165030)
XLA Ops:
  0.6 52.0 %spread.1 = (bf16[4,4,4,3,16,2048]{5,4,3,2,1,0:T(8,128)(2,1)}, bf16[2048,256]{1,0:T(8,128)(2,1)}, f32[16,8,256]{2,1,0:T(8,128)}, bf16[128,1024]{1,0:T(8,128)(2,1...) custom-call(bf16[4,3,16,2048]{3,2,1,0:T(8,128)(2,1)} %bitcast.25, f32[1,1,2048]{2,1,0:T(1,128)} %bitcast.36, ...), custom_call_target="tpu_custom_call" | custom-call | tf_op jit(solution)/shard_map/spread/pallas_call | solution.py:889
  52.6 40.3 %attend.1 = (bf16[3072,128]{1,0:T(8,128)(2,1)}, bf16[2,128,512]{2,1,0:T(8,128)(2,1)}) custom-call(s32[3]{0:T(128)} %lengths.1, s32[3,2,12]{2,1,0:T(2,128)} %bitcast.37, bf16[3072,2048]{1,0:T(8,128)(2,1)} %bitcast.20, bf16[3072,2048]{1,0:T(8,128)(2,1)} %bitcast.21, bf16[2048,128]{1,0:T(8,128)(2,1)} %bitcast.31, bf16[2048,256]{1,0:T(8,128)(2,1)} %get-tuple-element.13.wkv_ref, ...), custom_call_target="tpu_custom_call" | custom-call | tf_op jit(solution)/shard_map/attend/pallas_call | solution.py:928
  92.9 87.1 %middle.1 = (bf16[4,4,4,3,16,2048]{5,4,3,2,1,0:T(8,128)(2,1)}, f32[4,48,256]{2,1,0:T(8,128)}) custom-call(bf16[3072,128]{1,0:T(8,128)(2,1)} %get-tuple-element.15.heads_ref, bf16[128,2048]{1,0:T(8,128)(2,1)} %bitcast.28, bf16[128,1024]{1,0:T(8,128)(2,1)} %get-tuple-element.16.wo_pair_ref, bf16[4,3,16,2048]{3,2,1,0:T(8,128)(2,1)} %bitcast.26, f32[1,2048]{1,0:T(1,128)} %bitcast.35), custom_call_target="tpu_custom_call" | custom-call | tf_op jit(solution)/shard_map/middle/pallas_call | solution.py:952
  180.0 20.6 %hidden.1.hidden_ref = bf16[3072,352]{1,0:T(8,128)(2,1)} custom-call(bf16[3072,2048]{1,0:T(8,128)(2,1)} %bitcast.22, bf16[2048,768]{1,0:T(8,128)(2,1)} %get-tuple-element.18.weights_ref, f32[16,8,256]{2,1,0:T(8,128)} %get-tuple-element.14.routes_ref), custom_call_target="tpu_custom_call" | custom-call | tf_op jit(solution)/shard_map/hidden/pallas_call | solution.py:976
  200.5 52.3 %last.1 = bf16[192,256]{1,0:T(8,128)(2,1)} custom-call(bf16[3072,352]{1,0:T(8,128)(2,1)} %hidden.1.hidden_ref, bf16[352,2048]{1,0:T(8,128)(2,1)} %bitcast.24, bf16[352,1024]{1,0:T(8,128)(2,1)} %get-tuple-element.19.wd_pair_ref, f32[192,256]{1,0:T(8,128)} %bitcast.32), custom_call_target="tpu_custom_call" | custom-call | tf_op jit(solution)/shard_map/last/pallas_call | solution.py:989
  252.8 1.5 copy.19
